TPU v7x, 512 devices: a whole 4x4x16 slice. The times are simulated.
512 devices in a mesh: tm: 128 (over x, z, core), space: 4 (over y).
Axes of the slice: x: 4, y: 4, z: 16, core: 2. Of those that a mesh axis runs over, the one named last changes fastest.
Arguments:
- guess: float32 [128, 1, 64, 4096], P('tm', None, None, 'space'), may hold values from -6 to 6
- kernels: bfloat16 [256, 64, 576], P('tm'), may hold values from -0.25 to 0.25
- biases: float32 [256, 64], P('tm'), may hold values from -6 to 6
- probes: bfloat16 [2, 1, 64, 4096], P(None, None, None, 'space'), may hold values from -6 to 6
Outputs:
- states: float32 [128, 1, 64, 4096], P('tm', None, None, 'space')
- log_change: float32 [256], P('tm')
All inputs are finite; a program needn't handle non-finite values.
Results may differ from a plain program's by a relative error of at most 0.0018.
Values may be sent and summed in bfloat16 or wider, within the bound.
No kernel may reach another device: no remote copies, remote signals or barrier semaphores. Data moves between devices by JAX's collectives and lax.ppermute only.
A program may use at most 128 MiB of HBM per device.

v0:
```python
import jax
import jax.numpy as jnp
from jax import lax
from jax.sharding import Mesh
from jax.sharding import PartitionSpec as P

WIDTH = 64
TM = ("tm_0", "tm_1", "tm_2")


step_size = 0.0078125
highest = lax.Precision.HIGHEST


def extended(block, sides, width):
    for axis, dim in sides:
        count = lax.axis_size(axis)
        forward = [(i, i + 1) for i in range(count - 1)]
        backward = [(target, source) for source, target in forward]
        low = lax.ppermute(
            lax.slice_in_dim(block, block.shape[dim] - width, None, axis=dim), axis, forward
        )
        high = lax.ppermute(lax.slice_in_dim(block, 0, width, axis=dim), axis, backward)
        block = jnp.concatenate([low, block, high], axis=dim)
    return block


def copy_for_each(shard, axis):
    peers = lax.axis_size(axis)
    return lax.all_to_all(
        jnp.broadcast_to(shard[None], (peers, *shard.shape)), axis, 0, 0, tiled=True
    )


def taken_together(shard, axis):
    return copy_for_each(shard, axis).sum(axis=0)


def nothing_yet(shard, identity):
    return jax.tree.map(
        lambda part, zero: jnp.zeros_like(part) + jnp.asarray(zero, part.dtype), shard, identity
    )


def prefix_by_axis(shard, axes, combine, identity):
    before = start = nothing_yet(shard, identity)
    running = shard
    for axis in reversed(axes):
        peers, index = (lax.axis_size(axis), lax.axis_index(axis))
        pieces = jax.tree.map(lambda part: lax.all_gather(part, axis), running)
        inside, running = (start, start)
        for k in range(peers):
            passed = k < index
            running = combine(running, jax.tree.map(lambda part: part[k], pieces))
            inside = jax.tree.map(lambda new, old: jnp.where(passed, new, old), running, inside)
        before = combine(inside, before)
    return before


def gather_taps(stacked, row_len):
    out_rows = stacked.shape[2] // row_len - 2
    out_cells = out_rows * row_len
    padded = jnp.pad(stacked, ((0, 0), (0, 0), (1, 1)))
    column = jnp.arange(out_cells, dtype=jnp.int32) % row_len
    pieces = []
    for row_off in (-1, 0, 1):
        for col_off in (-1, 0, 1):
            offset = (1 + row_off) * row_len + col_off + 1
            window = padded[:, :, offset : offset + out_cells]
            if col_off == -1:
                window = jnp.where(column != 0, window, jnp.zeros_like(window))
            elif col_off == 1:
                window = jnp.where(column != row_len - 1, window, jnp.zeros_like(window))
            pieces.append(window)
    return jnp.concatenate(pieces, axis=1)


def mix_channels(matrix, field):
    return jnp.einsum("ij,bjn->bin", matrix, field, precision=highest)


def compose(earlier, later):
    return (
        jnp.dot(later[0], earlier[0], precision=highest),
        mix_channels(later[0], earlier[1]) + later[1],
    )


def accumulate(earlier, later):
    return earlier + later


def body(guess, kernels, biases, probes):
    row_len = WIDTH
    cells = guess.shape[3]
    images = guess.shape[1]
    rows = cells // row_len
    layers = kernels.shape[0]
    channels = kernels.shape[1]
    probe_count = probes.shape[0]
    strip = lax.axis_index("space")
    strips = lax.axis_size("space")
    position = lax.axis_index(TM)
    probe_ext = extended(probes, (("space", 3),), layers * row_len)
    probe_mid = probe_ext[:, :, :, layers * row_len : (layers + rows) * row_len].astype(jnp.float32)
    current = extended(guess[0], (("space", 2),), layers * row_len)
    partials = []
    for layer_index in range(layers):
        extent = layers - layer_index
        widened = current
        ext_cells = (rows + 2 * extent) * row_len
        global_row = strip * rows + jnp.arange(ext_cells, dtype=jnp.int32) // row_len - extent
        inside = (global_row >= 0) & (global_row < rows * strips)
        activation = jnp.where(inside, jnp.tanh(widened), 0.0)
        slopes = 1.0 - activation * activation
        start_cell = (layers - extent) * row_len
        probe_win = lax.slice_in_dim(probe_ext, start_cell, start_cell + ext_cells, axis=3).astype(
            jnp.float32
        )
        inputs = jnp.concatenate(
            [activation[0][None], slopes[0][None] * probe_win[:, 0]], axis=0
        ).astype(jnp.bfloat16)
        stacked = gather_taps(inputs, row_len)
        mixing = jnp.einsum(
            "ok,skn->son", kernels[layer_index], stacked, preferred_element_type=jnp.float32
        )
        forcing = mixing[0] + biases[layer_index][:, None]
        advanced = [widened[0, :, row_len : ext_cells - row_len] + step_size * forcing]
        inner = mixing[1:, :, (extent - 1) * row_len : (extent - 1 + rows) * row_len]
        partial_value = jnp.sum(probe_mid[:, 0] * inner)
        current = jnp.stack(advanced)
        partial_value = partial_value / (probe_count * images)
        partials.append(partial_value)
    traces = jnp.stack(partials)
    traces = taken_together(traces, "space")
    kernel_sum = kernels.astype(jnp.float32).reshape(layers, channels, 9, channels).sum(axis=(0, 2))
    identity = jnp.eye(channels, dtype=jnp.float32)
    matrix = identity + step_size * kernel_sum
    leading = position == 0
    offset = current - mix_channels(matrix, guess[0])
    matrix_elem = jnp.where(leading, 0.0, matrix)
    offset_elem = jnp.where(leading, current, offset)
    prefix_matrix, prefix_offset = prefix_by_axis(
        (matrix_elem, offset_elem), TM, compose, (identity, jnp.zeros_like(current))
    )
    new_state = mix_channels(prefix_matrix, guess[0]) + prefix_offset
    earlier_total = prefix_by_axis(jnp.sum(traces), TM, accumulate, jnp.zeros((), jnp.float32))
    log_change = -(step_size / row_len) * (earlier_total + jnp.cumsum(traces))
    return (new_state[None], log_change)


def solution(mesh):
    finer = Mesh(
        mesh.devices.reshape(4, 16, 2, mesh.shape["space"]), ("tm_0", "tm_1", "tm_2", "space")
    )
    placed = (
        P(TM, None, None, "space"),
        P(TM, None, None),
        P(TM, None),
        P(None, None, None, "space"),
    )
    return jax.shard_map(
        body,
        mesh=finer,
        in_specs=placed,
        out_specs=(P(TM, None, None, "space"), P(TM)),
        check_vma=False,
    )
```

profile of v0, /device:TPU:8, one launch (start us, length us, event | category | flops | bytes accessed | tf_op | source)
XLA Modules:
  0.0 232.1 jit_solution(13394516427415140937)
XLA Ops:
  7.2 0.8 fusion.293
  8.0 3.5 %collective-permute-start = (f32[1,64,128]{2,1,0:T(8,128)S(1)}, f32[1,64,128]{2,1,0:T(8,128)S(1)}, u32[]{:S(2)}, u32[]{:S(2)}) collective-permute-start(f32[1,64,128]{2,1,0:T(8,128)S(1)} %get-tuple-element.12), channel_id=1, source_target_pairs={{0,1},{1,2},{2,3},{4,5},{5,6},{6,7},{8,9},{9,10},{10,11},{12,13},{... | collective-permute-start | bytes 98312 | tf_op jit(solution)/shard_map/ppermute | solution.py:20
  11.5 5.5 %collective-permute-start.1 = (f32[1,64,128]{2,1,0:T(8,128)S(1)}, f32[1,64,128]{2,1,0:T(8,128)S(1)}, u32[]{:S(2)}, u32[]{:S(2)}) collective-permute-start(f32[1,64,128]{2,1,0:T(8,128)S(1)} %get-tuple-element.13), channel_id=1, source_target_pairs={{1,0},{2,1},{3,2},{5,4},{6,5},{7,6},{9,8},{10,9},{11,10},{13,12},{... | collective-permute-start | bytes 98312 | tf_op jit(solution)/shard_map/ppermute | solution.py:23
  17.0 0.8 fusion.292
  17.8 1.9 collective-permute-start.2
  19.7 3.9 %collective-permute-start.3 = (bf16[2,1,64,128]{3,2,0,1:T(8,128)(2,1)S(1)}, bf16[2,1,64,128]{3,2,0,1:T(8,128)(2,1)S(1)}, u32[]{:S(2)}, u32[]{:S(2)}) collective-permute-start(bf16[2,1,64,128]{3,2,0,1:T(8,128)(2,1)S(1)} %get-tuple-element.11), channel_id=1, source_target_pairs={{1,0},{2,1},{3,2},{5,4},{6,5},{7,6},{9,8},{10,9},{11,10},{13,12},{... | collective-permute-start | bytes 98312 | tf_op jit(solution)/shard_map/ppermute | solution.py:23
  23.7 0.8 slice_bitcast_fusion.5
  24.5 1.0 convert_reduce_fusion
  25.7 1.9 all_gather.52
  27.7 1.0 fusion.75
  28.7 1.0 multiply_convert_fusion
  29.8 1.0 pad_maximum_fusion.2
  32.4 0.8 convolution_bitcast_fusion
  35.1 0.8 convolution_bitcast_fusion.1
  35.9 0.4 fusion.4
  36.3 2.2 all-gather.2
  38.5 0.8 copy-done.15
  39.3 1.2 fusion.5
  40.5 1.3 dynamic-slice
  41.8 1.3 dynamic-slice.1
  43.4 37.8 %all-gather = f32[1024,64]{1,0:T(8,128)S(1)} all-gather(f32[64,64]{1,0:T(8,128)S(1)} %fusion.184), channel_id=2, replica_groups=mesh['tm_0'=4,'tm_1'=16,'tm_2'=2,'space'=4] {'tm_1'}, dimensions={0}, use_global_device_ids=true | all-gather | bytes 278528 | tf_op jit(solution)/shard_map/all_gather | solution.py:50
  83.9 13.4 %all-gather.1 = f32[256,64]{1,0:T(8,128)S(1)} all-gather(f32[64,64]{1,0:T(8,128)S(1)} %fusion.237), channel_id=3, replica_groups=mesh['tm_0'=4,'tm_1'=16,'tm_2'=2,'space'=4] {'tm_0'}, dimensions={0}, use_global_device_ids=true | all-gather | bytes 81920 | tf_op jit(solution)/shard_map/all_gather | solution.py:50
  98.5 0.6 copy-done.20
  99.0 0.8 fusion.297
  99.8 21.1 %all-gather.8.cloned.1.call-done = f32[16,64,1024]{2,1,0:T(8,128)} async-done(((f32[1,64,1024]{2,1,0:T(8,128)}), f32[16,64,1024]{2,1,0:T(8,128)}) %all-gather.8.cloned.1.call-update) | async-done | bytes 4194320 | tf_op jit(solution)/shard_map/all_gather | solution.py:50
  120.9 1.6 fusion.6
  122.6 1.3 fusion.7
  123.9 1.3 fusion.8
  125.2 1.3 fusion.9
  126.5 1.4 fusion.10
  128.0 0.7 copy-done.4
  128.7 1.3 fusion.11
  130.0 0.7 copy-done.5
  131.1 0.7 copy-done.6
  131.8 0.4 fusion.13
  132.2 0.7 copy-done.7
  133.3 0.7 copy-done.8
  134.4 0.7 copy-done.9
  135.5 0.7 copy-done.10
  136.5 0.7 copy-done.11
  137.6 0.7 copy-done.12
  138.7 0.7 copy-done.13
  139.4 1.1 fusion.20
  140.5 1.1 convolution_bitcast_fusion.22
  141.7 0.8 fusion.27
  143.8 8.4 %all_to_all.6 = f32[4,1,2]{2,1,0:T(1,128)S(1)} all-to-all(f32[4,1,2]{2,1,0:T(1,128)S(1)} %broadcast_in_dim.87), channel_id=1, replica_groups=mesh['tm_0'=4,'tm_1'=16,'tm_2'=2,'space'=4] {'space'}, dimensions={0} | all-to-all | bytes 64 | tf_op jit(solution)/shard_map/all_to_all | solution.py:30
  152.3 0.6 fusion.290
  152.9 1.4 dynamic-update-slice
  154.2 1.3 dynamic-slice.2
  155.5 2.4 %all-reduce.2 = f32[2]{0:T(128)S(1)} all-reduce(f32[2]{0:T(128)S(1)} %dynamic-update-slice), channel_id=1, replica_groups=mesh['tm_0'=4,'tm_1'=16,'tm_2'=2,'space'=4] {'tm_2'}, use_global_device_ids=true, to_apply=%add.2 | all-reduce | flops 2 | bytes 16
  158.0 0.6 fusion.296
  159.8 0.7 dynamic-update-slice.1
  160.4 29.1 %all-reduce.3 = f32[16]{0:T(128)S(1)} all-reduce(f32[16]{0:T(128)S(1)} %dynamic-update-slice.1), channel_id=1, replica_groups=mesh['tm_0'=4,'tm_1'=16,'tm_2'=2,'space'=4] {'tm_1'}, use_global_device_ids=true, to_apply=%add.3 | all-reduce | flops 16 | bytes 128
  189.5 0.7 fusion.295
  200.4 0.7 dynamic-update-slice.2
  201.1 0.9 multiply_reduce_fusion.2
  201.9 10.5 %all-reduce.4 = f32[4]{0:T(128)S(1)} all-reduce(f32[4]{0:T(128)S(1)} %dynamic-update-slice.2), channel_id=1, replica_groups=mesh['tm_0'=4,'tm_1'=16,'tm_2'=2,'space'=4] {'tm_0'}, use_global_device_ids=true, to_apply=%add.4 | all-reduce | flops 4 | bytes 32
  213.6 0.6 fusion.294
  217.4 0.5 multiply_bitcast_fusion
  217.9 1.6 fusion.82
  219.6 1.5 fusion.21
  221.1 1.3 fusion.22
  222.4 1.4 fusion.25
  224.2 1.1 fusion.2
  (114 shorter events, 11.2 us)
Async XLA Ops:
  7.2 113.8 %all-gather.8.cloned.1.call-start = ((), (), s32[]{:S(2)}) async-start(), calls=%async_computation.1 | async-start | bytes 4456448 | tf_op jit(solution)/shard_map/all_gather | solution.py:50
  8.0 19.7 %collective-permute-start = (f32[1,64,128]{2,1,0:T(8,128)S(1)}, f32[1,64,128]{2,1,0:T(8,128)S(1)}, u32[]{:S(2)}, u32[]{:S(2)}) collective-permute-start(f32[1,64,128]{2,1,0:T(8,128)S(1)} %get-tuple-element.12), channel_id=1, source_target_pairs={{0,1},{1,2},{2,3},{4,5},{5,6},{6,7},{8,9},{9,10},{10,11},{12,13},{... | collective-permute-start | bytes 98312 | tf_op jit(solution)/shard_map/ppermute | solution.py:20
  11.5 16.2 %collective-permute-start.1 = (f32[1,64,128]{2,1,0:T(8,128)S(1)}, f32[1,64,128]{2,1,0:T(8,128)S(1)}, u32[]{:S(2)}, u32[]{:S(2)}) collective-permute-start(f32[1,64,128]{2,1,0:T(8,128)S(1)} %get-tuple-element.13), channel_id=1, source_target_pairs={{1,0},{2,1},{3,2},{5,4},{6,5},{7,6},{9,8},{10,9},{11,10},{13,12},{... | collective-permute-start | bytes 98312 | tf_op jit(solution)/shard_map/ppermute | solution.py:23
  17.8 10.9 %collective-permute-start.2 = (bf16[2,1,64,128]{3,2,0,1:T(8,128)(2,1)S(1)}, bf16[2,1,64,128]{3,2,0,1:T(8,128)(2,1)S(1)}, u32[]{:S(2)}, u32[]{:S(2)}) collective-permute-start(bf16[2,1,64,128]{3,2,0,1:T(8,128)(2,1)S(1)} %get-tuple-element.10), channel_id=1, source_target_pairs={{0,1},{1,2},{2,3},{4,5},{5,6},{6,7},{8,9},{9,10},{10,11},{12,13},{... | collective-permute-start | bytes 98312 | tf_op jit(solution)/shard_map/ppermute | solution.py:20
  19.7 9.0 %collective-permute-start.3 = (bf16[2,1,64,128]{3,2,0,1:T(8,128)(2,1)S(1)}, bf16[2,1,64,128]{3,2,0,1:T(8,128)(2,1)S(1)}, u32[]{:S(2)}, u32[]{:S(2)}) collective-permute-start(bf16[2,1,64,128]{3,2,0,1:T(8,128)(2,1)S(1)} %get-tuple-element.11), channel_id=1, source_target_pairs={{1,0},{2,1},{3,2},{5,4},{6,5},{7,6},{9,8},{10,9},{11,10},{13,12},{... | collective-permute-start | bytes 98312 | tf_op jit(solution)/shard_map/ppermute | solution.py:23
  30.8 1.6 copy-start.19
  32.2 1.2 copy-start.2
  34.5 1.4 copy-start
  38.5 0.8 copy-start.15
  40.5 179.1 %all-gather.10.cloned.1.call-start = ((), (), s32[]{:S(2)}) async-start(), calls=%async_computation.2 | async-start | bytes 1310720 | tf_op jit(solution)/shard_map/all_gather | solution.py:50
  97.3 0.8 copy-start.17
  98.4 0.6 copy-start.20
  120.9 9.8 %copy-start.1 = (f32[16,64,1024]{2,1,0:T(8,128)S(1)}, f32[16,64,1024]{2,1,0:T(8,128)}, u32[]{:S(2)}) copy-start(f32[16,64,1024]{2,1,0:T(8,128)} %all-gather.8.cloned.1.call-done) | copy-start | bytes 12582916
  126.5 12.2 %copy-start.3 = (f32[1,64,1024]{2,1,0:T(8,128)}, f32[1,64,1024]{2,1,0:T(8,128)S(1)}, u32[]{:S(2)}) copy-start(f32[1,64,1024]{2,1,0:T(8,128)S(1)} %fusion.9) | copy-start | bytes 786436
  128.0 0.7 copy-start.4
  130.0 0.7 copy-start.5
  131.1 0.7 copy-start.6
  132.2 0.7 copy-start.7
  133.3 0.7 copy-start.8
  134.4 0.7 copy-start.9
  135.4 0.7 copy-start.10
  136.5 0.7 copy-start.11
  137.6 0.7 copy-start.12
  138.7 0.7 copy-start.13
  140.5 79.1 %copy-start.18 = (f32[256,64]{1,0:T(8,128)S(1)}, f32[256,64]{1,0:T(8,128)}, u32[]{:S(2)}) copy-start(f32[256,64]{1,0:T(8,128)} %copy-done.17) | copy-start | bytes 196612
  141.7 82.1 %copy-start.21 = (f32[64,64]{1,0:T(8,128)S(1)}, f32[64,64]{1,0:T(8,128)}, u32[]{:S(2)}) copy-start(f32[64,64]{1,0:T(8,128)} %copy-done.20) | copy-start | bytes 49156
  142.5 81.7 %copy-start.14 = (f32[1,64,1024]{2,1,0:T(8,128)S(1)}, f32[1,64,1024]{2,1,0:T(8,128)}, u32[]{:S(2)}) copy-start(f32[1,64,1024]{2,1,0:T(8,128)} %fusion.5) | copy-start | bytes 786436
  142.5 81.7 %copy-start.16 = (f32[2,64,1024]{2,1,0:T(8,128)S(1)}, f32[2,64,1024]{2,1,0:T(8,128)}, u32[]{:S(2)}) copy-start(f32[2,64,1024]{2,1,0:T(8,128)} %copy-done.15) | copy-start | bytes 1572868
Sparse Core Ops, SparseCore 0:
  40.6 80.2 all-gather.7
  140.6 27.0 all-gather.9
where the time goes:
time: 233 us; the launch traced here: 232 us
  blocking collectives  106 us (45%)
  between operations  31.7 us (14%)
  matrix products  28.5 us (12%)
  waiting for transfers between devices  21.2 us (9%)
  local copies, waits for them, and re-layouts  19.6 us (8%)
  starting transfers between devices  14.9 us (6%)
  other arithmetic  10.7 us (5%)
    all_gather x4, blocking collectives, prefix_by_axis(): pieces = jax.tree.map(lambda part: lax.all_gather(part, axis), running)  55.2 us
    unnamed x3, blocking collectives  42 us
    dot_general x24, matrix products, mix_channels(): return jnp.einsum('ij,bjn->bin', matrix, field, precision=highest)  22.3 us
    all_gather x2, waiting for transfers between devices, prefix_by_axis(): pieces = jax.tree.map(lambda part: lax.all_gather(part, axis), running)  21.1 us
    unnamed x53, local copies, waits for them, and re-layouts  15.1 us
    ppermute x2, starting transfers between devices, extended(): lax.ppermute(lax.slice_in_dim(block, 0, width, axis=dim), axis, backward)  9.43 us
    all_to_all x1, blocking collectives, copy_for_each(): lax.all_to_all(jnp.broadcast_to(shard[None], (peers, *shard.shape)), axis...  8.43 us
    ppermute x2, starting transfers between devices, extended(): lax.ppermute(lax.slice_in_dim(block, block.shape[dim] - width, None, axis...  5.38 us
  transfers between devices with their start and end apart: 6, of which 1 were waited for; matrix products, arithmetic and copies ran while one was open for 10% of the time, Pallas kernels for 0%

commit v1 on v0

v1 whole, which is shorter than its diff:
```python
import functools

import jax
import jax.numpy as jnp
from jax import lax
from jax.experimental import pallas as pl
from jax.experimental.pallas import tpu as pltpu
from jax.sharding import Mesh
from jax.sharding import PartitionSpec as P

WIDTH = 64
STEP = 0.0078125
TM = ("x", "zh", "zl", "c")
NEAR = ("zl", "c")
F32 = jnp.float32
BF16 = jnp.bfloat16


def split3(m):
    hi = m.astype(BF16)
    return hi, (m - hi.astype(F32)).astype(BF16)


def left3(m):
    hi, lo = split3(m)
    return jnp.concatenate([hi, hi, lo], axis=1)


def right3(v):
    hi, lo = split3(v)
    return jnp.concatenate([hi, lo, hi], axis=0)


def mix(m, v):
    return jnp.dot(left3(m), right3(v), preferred_element_type=F32)


def fold(m):
    half = m.shape[0] // 2
    return jnp.concatenate([m[:half], m[half:]], axis=1)


def unfold(m):
    half = m.shape[1] // 2
    return jnp.concatenate([m[:, :half], m[:, half:]], axis=0)


def eye(n):
    return (
        lax.broadcasted_iota(jnp.int32, (n, n), 0) == lax.broadcasted_iota(jnp.int32, (n, n), 1)
    ).astype(F32)


def edge_kernel(g_first, g_last, p_first, p_last, up_ref, down_ref):
    up_ref[:64] = g_first[0, 0]
    down_ref[:64] = g_last[0, 0]
    first = [p_first[n, 0].astype(F32)[:, :WIDTH] for n in range(2)]
    last = [p_last[n, 0].astype(F32)[:, WIDTH:] for n in range(2)]
    up_ref[64:] = jnp.concatenate(first, axis=1)
    down_ref[64:] = jnp.concatenate(last, axis=1)


def edges(guess, probes):
    last = guess.shape[3] // 128 - 1
    g_block, p_block = (1, 1, 64, 128), (2, 1, 64, 128)
    return pl.pallas_call(
        edge_kernel,
        grid=(1,),
        in_specs=[
            pl.BlockSpec(g_block, lambda i: (0, 0, 0, 0)),
            pl.BlockSpec(g_block, lambda i: (0, 0, 0, last)),
            pl.BlockSpec(p_block, lambda i: (0, 0, 0, 0)),
            pl.BlockSpec(p_block, lambda i: (0, 0, 0, last)),
        ],
        out_specs=[pl.BlockSpec((128, 128), lambda i: (0, 0))] * 2,
        out_shape=[jax.ShapeDtypeStruct((128, 128), F32)] * 2,
        name="edges",
    )(guess, guess, probes, probes)


def taps(v, column):
    n = v.shape[1]
    left = pltpu.roll(jnp.where(column == WIDTH - 1, 0.0, v), 1, 1)
    right = pltpu.roll(jnp.where(column == 0, 0.0, v), n - 1, 1)
    rows = []
    for part in (left, v, right):
        above = pltpu.roll(part, WIDTH, 1)
        below = jnp.concatenate([above[:, 128:], above[:, :128]], axis=1)
        rows.append((above, part, below))
    return jnp.concatenate(
        [rows[dx][dy].astype(BF16) for dy in range(3) for dx in range(3)], axis=0
    )


def steps_kernel(place_ref, g_ref, low_ref, high_ref, p_ref, k_ref, b_ref, send_ref, t_ref):
    strip_first, strip_last, leading = place_ref[0] == 1, place_ref[1] == 1, place_ref[2] == 1
    g = g_ref[0, 0]
    cells = g.shape[1]
    wide = cells + 256
    lane = lax.broadcasted_iota(jnp.int32, (64, wide), 1)
    column = lane & (WIDTH - 1)
    outside = (strip_first & (lane < 128)) | (strip_last & (lane >= wide - 128))
    zero = jnp.zeros((64, WIDTH), F32)
    probe_mid = [p_ref[n, 0].astype(F32) for n in range(2)]
    probe = [
        jnp.concatenate(
            [
                zero,
                low_ref[64:, n * WIDTH : (n + 1) * WIDTH],
                probe_mid[n],
                high_ref[64:, n * WIDTH : (n + 1) * WIDTH],
                zero,
            ],
            axis=1,
        )
        for n in range(2)
    ]
    diagonal = eye(64) == 1.0
    current = jnp.concatenate([low_ref[:64], g, high_ref[:64]], axis=1)
    moved = jnp.zeros((64, cells), F32)
    rows = lax.broadcasted_iota(jnp.int32, (8, 128), 0)
    trace = jnp.zeros((8, 128), F32)
    for layer in range(2):
        kernel = k_ref[layer]
        bias = jnp.sum(
            jnp.where(diagonal, b_ref[layer : layer + 1, :], 0.0), axis=1, keepdims=True
        )
        activation = jnp.tanh(current)
        if layer:
            activation = jnp.where(outside, 0.0, activation)
        slopes = 1.0 - activation * activation
        stack = taps(activation.astype(BF16).astype(F32), column)
        if layer:
            stack = stack[:, 128 : 128 + cells]
        forcing = jnp.dot(kernel, stack, preferred_element_type=F32) + bias
        total = jnp.zeros((64, cells), F32)
        for n in range(2):
            stack = taps((slopes * probe[n]).astype(BF16).astype(F32), column)
            inner = jnp.dot(kernel, stack[:, 128 : 128 + cells], preferred_element_type=F32)
            total = total + probe_mid[n] * inner
        trace = jnp.where(rows == layer, 0.5 * jnp.sum(total), trace)
        if layer:
            moved = moved + STEP * forcing
        else:
            current = current + STEP * forcing
            moved = moved + STEP * forcing[:, 128 : 128 + cells]
    t_ref[...] = trace
    both = k_ref[0].astype(F32) + k_ref[1].astype(F32)
    pair = both[:, :128] + both[:, 128:256] + both[:, 256:384] + both[:, 384:512]
    coarse = STEP * (pair[:, :64] + pair[:, 64:] + both[:, 512:])
    offset = jnp.where(leading, moved + g, moved - mix(coarse, g))
    change = fold(jnp.where(leading, -eye(64), coarse))
    for j in range(cells // 128):
        send_ref[j, :64] = offset[:, j * 128 : (j + 1) * 128]
        send_ref[j, 64:] = change


def whole(*shape):
    return pl.BlockSpec(memory_space=pltpu.VMEM)


def scalars():
    return pl.BlockSpec(memory_space=pltpu.SMEM)


def call(kernel, shapes, places, args, name):
    return pl.pallas_call(
        kernel,
        in_specs=[scalars()] * places + [whole()] * (len(args) - places),
        out_specs=[whole()] * len(shapes),
        out_shape=[jax.ShapeDtypeStruct(s, F32) for s in shapes],
        name=name,
    )(*args)


def advance(matrix, value, change, offset):
    wide = jnp.concatenate([value, matrix], axis=1)
    moved = wide + mix(change, wide)
    return moved[:, 128:], moved[:, :128] + offset


def near_kernel(r_ref, t_ref, send_ref, value_ref, matrix_ref):
    count = r_ref.shape[0]
    matrix, value = eye(64), jnp.zeros((64, 128), F32)
    for j in range(count):
        value_ref[j] = value
        matrix_ref[j] = matrix
        matrix, value = advance(matrix, value, unfold(r_ref[j, 64:96]), r_ref[j, :64])
    change = fold(matrix - eye(64))
    for i in range(send_ref.shape[0]):
        send_ref[i, :64] = value
        send_ref[i, 64:96] = change
        send_ref[i, 96:] = t_ref[...]


def far_kernel(place_ref, r_ref, send_ref, value_ref, matrix_ref, t_ref):
    count = r_ref.shape[0]
    me = place_ref[0]
    rows = lax.broadcasted_iota(jnp.int32, (8, 128), 0)
    matrix, value = eye(64), jnp.zeros((64, 128), F32)
    own_matrix, own_value = matrix, value
    before = total = own = jnp.zeros((8, 128), F32)
    for i in range(count):
        own_matrix = jnp.where(me == i, matrix, own_matrix)
        own_value = jnp.where(me == i, value, own_value)
        t = r_ref[i, 96:]
        before = jnp.where(me == i, total, before)
        own = jnp.where(me == i, t, own)
        total = total + t
        matrix, value = advance(matrix, value, unfold(r_ref[i, 64:96]), r_ref[i, :64])
    value_ref[...] = own_value
    matrix_ref[...] = own_matrix
    spread = jnp.sum(before, axis=0, keepdims=True)
    t_ref[...] = jnp.where(rows == 2, spread, own)
    change = fold(matrix - eye(64))
    for i in range(send_ref.shape[0]):
        send_ref[i, :64] = value
        send_ref[i, 64:96] = change
        send_ref[i, 96:] = total


def back_kernel(place_ref, r_ref, far_value, far_matrix, t_ref, near_value, near_matrix, send_ref):
    me = place_ref[0]
    rows = lax.broadcasted_iota(jnp.int32, (8, 128), 0)
    state = own = jnp.zeros((64, 128), F32)
    before = total = jnp.zeros((8, 128), F32)
    count = r_ref.shape[0]
    for i in range(count):
        own = jnp.where(me == i, state, own)
        before = jnp.where(me == i, total, before)
        total = total + r_ref[i, 96:]
        if i < count - 1:
            state = state + mix(unfold(r_ref[i, 64:96]), state) + r_ref[i, :64]
    entry = mix(far_matrix[...], own) + far_value[...]
    near = near_matrix.shape[0]
    states = mix(near_matrix[...].reshape(near * 64, 64), entry)
    spread = jnp.sum(before, axis=0, keepdims=True)
    t = t_ref[...] + jnp.where(rows == 2, spread, 0.0)
    for j in range(near):
        send_ref[j, :64] = states[j * 64 : (j + 1) * 64] + near_value[j]
        send_ref[j, 64:] = t


def final_kernel(place_ref, r_ref, g_ref, state_ref, log_ref):
    leading, me = place_ref[0] == 1, place_ref[1]
    count = r_ref.shape[0]
    rows = lax.broadcasted_iota(jnp.int32, (8, 128), 0)
    earlier = jnp.zeros((1, 128), F32)
    own = jnp.zeros((8, 128), F32)
    for j in range(count):
        at = slice(j * 128, (j + 1) * 128)
        state_ref[0, 0, :, at] = jnp.where(leading, g_ref[0, 0, :, at], r_ref[j, :64])
        t = r_ref[j, 64:]
        earlier = earlier + t[2:3] + jnp.where(j < me, t[0:1] + t[1:2], 0.0)
        own = jnp.where(me == j, t, own)
    first = earlier + own[0:1]
    second = first + own[1:2]
    log_ref[...] = -(STEP / WIDTH) * jnp.where(rows == 0, first, second)


def body(guess, kernels, biases, probes):
    strips = lax.axis_size("space")
    strip = lax.axis_index("space")
    near = lax.axis_size("zl") * lax.axis_size("c")
    far, last = lax.axis_size("zh"), lax.axis_size("x")
    leading = (lax.axis_index(TM) == 0).astype(jnp.int32)
    cells = guess.shape[3]

    up, down = edges(guess, probes)
    forward = [(i, i + 1) for i in range(strips - 1)]
    backward = [(i + 1, i) for i in range(strips - 1)]
    low = lax.ppermute(down, "space", forward)
    high = lax.ppermute(up, "space", backward)

    place = jnp.stack(
        [(strip == 0).astype(jnp.int32), (strip == strips - 1).astype(jnp.int32), leading]
    )
    send, trace = call(
        steps_kernel,
        [(near, 96, 128), (8, 128)],
        1,
        (place, guess, low, high, probes, kernels, biases),
        "steps",
    )
    hop = 1
    while hop < strips:
        trace = trace + lax.ppermute(trace, "space", [(i, i ^ hop) for i in range(strips)])
        hop *= 2
    got = lax.all_to_all(send, NEAR, 0, 0, tiled=True)
    send, near_value, near_matrix = call(
        near_kernel,
        [(far, 104, 128), (near, 64, 128), (near, 64, 64)],
        0,
        (got, trace),
        "near",
    )
    got = lax.all_to_all(send, "zh", 0, 0, tiled=True)
    send, far_value, far_matrix, trace = call(
        far_kernel,
        [(last, 104, 128), (64, 128), (64, 64), (8, 128)],
        1,
        (lax.axis_index("zh").reshape(1), got),
        "far",
    )
    got = lax.all_to_all(send, "x", 0, 0, tiled=True)
    (send,) = call(
        back_kernel,
        [(near, 72, 128)],
        1,
        (lax.axis_index("x").reshape(1), got, far_value, far_matrix, trace, near_value, near_matrix),
        "back",
    )
    got = lax.all_to_all(send, NEAR, 0, 0, tiled=True)
    place = jnp.stack([leading, lax.axis_index(NEAR)])
    states, log_change = call(
        final_kernel, [(1, 1, 64, cells), (8, 128)], 1, (place, got, guess), "final"
    )
    return states, log_change[:2, 0]


def solution(mesh):
    finer = Mesh(
        mesh.devices.reshape(4, 4, 4, 2, mesh.shape["space"]), ("x", "zh", "zl", "c", "space")
    )
    placed = (
        P(TM, None, None, "space"),
        P(TM, None, None),
        P(TM, None),
        P(None, None, None, "space"),
    )
    return jax.shard_map(
        body,
        mesh=finer,
        in_specs=placed,
        out_specs=(P(TM, None, None, "space"), P(TM)),
        check_vma=False,
    )
```

time: 233 us -> 106 us (0.45)
  the two profiles are of different devices: /device:TPU:8 before, /device:TPU:1 now
where the time goes in v1:
time: 106 us; the launch traced here: 105 us
  blocking collectives  35.2 us (33%)
  starting transfers between devices  31.8 us (30%)
  waiting for transfers between devices  16.5 us (16%)
  Pallas kernels  16 us (15%)
  local copies, waits for them, and re-layouts  3.39 us (3%)
  other arithmetic  1.81 us (2%)
    all_to_all x1, blocking collectives, body(): got = lax.all_to_all(send, 'zh', 0, 0, tiled=True)  25.8 us
    all_to_all x2, starting transfers between devices, body(): got = lax.all_to_all(send, NEAR, 0, 0, tiled=True)  20 us
    pallas_call x5, Pallas kernels, call(): pl.pallas_call(kernel, in_specs=[scalars()] * places + [whole()] * (len(a...  14.5 us
    all_to_all x1, blocking collectives, body(): got = lax.all_to_all(send, 'x', 0, 0, tiled=True)  9.38 us
    all_to_all x2, waiting for transfers between devices, body(): got = lax.all_to_all(send, NEAR, 0, 0, tiled=True)  9.26 us
    ppermute x2, starting transfers between devices, body(): lax.ppermute(trace, 'space', [(i, i ^ hop) for i in range(strips)])  6.5 us
    ppermute x1, starting transfers between devices, body(): low = lax.ppermute(down, 'space', forward)  4.01 us
    ppermute x2, waiting for transfers between devices, body(): lax.ppermute(trace, 'space', [(i, i ^ hop) for i in range(strips)])  3.97 us
  transfers between devices with their start and end apart: 6, of which 5 were waited for; matrix products, arithmetic and copies ran while one was open for 2% of the time, Pallas kernels for 0%

profile of v1, /device:TPU:1, one launch (start us, length us, event | category | flops | bytes accessed | tf_op | source)
XLA Modules:
  0.0 105.5 jit_solution(18264083314917679907)
XLA Ops:
  0.6 1.5 %edges.1 = (f32[128,128]{1,0:T(8,128)}, f32[128,128]{1,0:T(8,128)}) custom-call(f32[1,1,64,1024]{3,2,1,0:T(8,128)} %g_ref.3, f32[1,1,64,1024]{3,2,1,0:T(8,128)} %g_ref.3, bf16[2,1,64,1024]{3,2,1,0:T(8,128)(2,1)} %p_ref.1, bf16[2,1,64,1024]{3,2,1,0:T(8,128)(2,1)} %p_ref.1), custom_call_target="tpu_custom_call" | custom-call | tf_op jit(solution)/shard_map/edges/pallas_call | solution.py:66
  2.2 4.0 %collective-permute-start = (f32[128,128]{1,0:T(8,128)}, f32[128,128]{1,0:T(8,128)S(1)}, u32[]{:S(2)}, u32[]{:S(2)}) collective-permute-start(f32[128,128]{1,0:T(8,128)} %get-tuple-element.15), channel_id=1, source_target_pairs={{0,1},{1,2},{2,3},{4,5},{5,6},{6,7},{8,9},{9,10},{10,11},{12,13},{... | collective-permute-start | bytes 196616 | tf_op jit(solution)/shard_map/ppermute | solution.py:272
  6.2 1.3 %collective-permute-start.1 = (f32[128,128]{1,0:T(8,128)}, f32[128,128]{1,0:T(8,128)S(1)}, u32[]{:S(2)}, u32[]{:S(2)}) collective-permute-start(f32[128,128]{1,0:T(8,128)} %get-tuple-element.16), channel_id=1, source_target_pairs={{1,0},{2,1},{3,2},{5,4},{6,5},{7,6},{9,8},{10,9},{11,10},{13,12},{... | collective-permute-start | bytes 196616 | tf_op jit(solution)/shard_map/ppermute | solution.py:273
  7.5 0.6 pad_add_fusion.1.place_ref
  8.1 0.0 collective-permute-done.low_ref
  8.1 0.0 copy-start.2
  8.1 3.3 %collective-permute-done.1.high_ref = f32[128,128]{1,0:T(8,128)S(1)} collective-permute-done((f32[128,128]{1,0:T(8,128)}, f32[128,128]{1,0:T(8,128)S(1)}, u32[]{:S(2)}, u32[]{:S(2)}) %collective-permute-start.1) | collective-permute-done | bytes 65568 | tf_op jit(solution)/shard_map/ppermute | solution.py:273
  11.4 0.0 copy-done.2
  11.4 0.0 copy-start.3
  11.4 0.6 copy-done.3
  12.0 4.5 %steps.1 = (f32[8,96,128]{2,1,0:T(8,128)}, f32[8,128]{1,0:T(8,128)}) custom-call(s32[3]{0:T(128)} %pad_add_fusion.1.place_ref, f32[1,1,64,1024]{3,2,1,0:T(8,128)} %g_ref.3, f32[128,128]{1,0:T(8,128)} %copy-done.2, f32[128,128]{1,0:T(8,128)} %copy-done.3, bf16[2,1,64,1024]{3,2,1,0:T(8,128)(2,1)} %p_ref.1, bf16[2,64,576]{2,1,0:T(8,128)(2,1)} %k_ref.1, ...), custom_call_target="tpu_custom_call" | custom-call | tf_op jit(solution)/shard_map/steps/pallas_call | solution.py:167
  16.5 0.0 copy-start.4
  16.5 8.7 %all-to-all-start = ((f32[8,96,128]{2,1,0:T(8,128)}), f32[8,96,128]{2,1,0:T(8,128)S(1)}, u32[]{:S(2)}, u32[]{:S(2)}) async-start(f32[8,96,128]{2,1,0:T(8,128)} %get-tuple-element.17), calls=%async_computation | async-start | bytes 786432 | tf_op jit(solution)/shard_map/all_to_all | solution.py:289
  25.2 0.0 copy-done.4
  25.2 2.6 %collective-permute-start.2 = (f32[8,128]{1,0:T(8,128)S(1)}, f32[8,128]{1,0:T(8,128)S(1)}, u32[]{:S(2)}, u32[]{:S(2)}) collective-permute-start(f32[8,128]{1,0:T(8,128)S(1)} %copy-done.4), channel_id=1, source_target_pairs={{0,1},{1,0},{2,3},{3,2},{4,5},{5,4},{6,7},{7,6},{8,9},{9,8},{10,11... | collective-permute-start | bytes 12296 | tf_op jit(solution)/shard_map/ppermute | solution.py:287
  27.8 2.0 %collective-permute-done.2 = f32[8,128]{1,0:T(8,128)S(1)} collective-permute-done((f32[8,128]{1,0:T(8,128)S(1)}, f32[8,128]{1,0:T(8,128)S(1)}, u32[]{:S(2)}, u32[]{:S(2)}) %collective-permute-start.2) | collective-permute-done | bytes 4128 | tf_op jit(solution)/shard_map/ppermute | solution.py:287
  29.9 3.9 %collective-permute-start.3 = (f32[8,128]{1,0:T(8,128)S(1)}, f32[8,128]{1,0:T(8,128)S(1)}, u32[]{:S(2)}, u32[]{:S(2)}) collective-permute-start(f32[8,128]{1,0:T(8,128)S(1)} %add.19), channel_id=1, source_target_pairs={{0,2},{1,3},{2,0},{3,1},{4,6},{5,7},{6,4},{7,5},{8,10},{9,11},{10,... | collective-permute-start | bytes 12296 | tf_op jit(solution)/shard_map/ppermute | solution.py:287
  33.8 1.9 %collective-permute-done.3 = f32[8,128]{1,0:T(8,128)S(1)} collective-permute-done((f32[8,128]{1,0:T(8,128)S(1)}, f32[8,128]{1,0:T(8,128)S(1)}, u32[]{:S(2)}, u32[]{:S(2)}) %collective-permute-start.3) | collective-permute-done | bytes 4128 | tf_op jit(solution)/shard_map/ppermute | solution.py:287
  35.7 0.6 add.20.t_ref
  36.3 0.5 all-to-all-done.r_ref
  36.9 0.0 copy-start
  36.9 0.7 copy-done
  37.6 3.1 %near.1 = (f32[4,104,128]{2,1,0:T(8,128)}, f32[8,64,128]{2,1,0:T(8,128)}, f32[8,64,64]{2,1,0:T(8,128)}) custom-call(f32[8,96,128]{2,1,0:T(8,128)} %copy-done, f32[8,128]{1,0:T(8,128)} %add.20.t_ref), custom_call_target="tpu_custom_call" | custom-call | tf_op jit(solution)/shard_map/near/pallas_call | solution.py:167
  40.7 25.8 %all_to_all.20.r_ref = f32[4,104,128]{2,1,0:T(8,128)} all-to-all(f32[4,104,128]{2,1,0:T(8,128)} %get-tuple-element.19), channel_id=1, replica_groups=mesh['x'=4,'zh'=4,'zl'=4,'c'=2,'space'=4] {'zh'}, dimensions={0} | all-to-all | bytes 425984 | tf_op jit(solution)/shard_map/all_to_all | solution.py:297
  66.5 2.4 %far.1 = (f32[4,104,128]{2,1,0:T(8,128)}, f32[64,128]{1,0:T(8,128)}, f32[64,64]{1,0:T(8,128)}, f32[8,128]{1,0:T(8,128)}) custom-call(s32[1]{0:T(128)} %bitcast.3.place_ref, f32[4,104,128]{2,1,0:T(8,128)} %all_to_all.20.r_ref), custom_call_target="tpu_custom_call" | custom-call | tf_op jit(solution)/shard_map/far/pallas_call | solution.py:167
  68.9 9.4 %all_to_all.21.r_ref = f32[4,104,128]{2,1,0:T(8,128)} all-to-all(f32[4,104,128]{2,1,0:T(8,128)} %get-tuple-element.20), channel_id=1, replica_groups=mesh['x'=4,'zh'=4,'zl'=4,'c'=2,'space'=4] {'x'}, dimensions={0} | all-to-all | bytes 425984 | tf_op jit(solution)/shard_map/all_to_all | solution.py:305
  78.3 2.8 %back.1 = f32[8,72,128]{2,1,0:T(8,128)} custom-call(s32[1]{0:T(128)} %bitcast.2.place_ref, f32[4,104,128]{2,1,0:T(8,128)} %all_to_all.21.r_ref, f32[64,128]{1,0:T(8,128)} %get-tuple-element.21.far_value, f32[64,64]{1,0:T(8,128)} %get-tuple-element.22.far_matrix, f32[8,128]{1,0:T(8,128)} %get-tuple-element.23.t_ref, ...), custom_call_target="tpu_custom_call" | custom-call | tf_op jit(solution)/shard_map/back/pallas_call | solution.py:167
  81.1 11.3 %all-to-all-start.3 = ((f32[8,72,128]{2,1,0:T(8,128)}), f32[8,72,128]{2,1,0:T(8,128)S(1)}, u32[]{:S(2)}, u32[]{:S(2)}) async-start(f32[8,72,128]{2,1,0:T(8,128)} %back.1), calls=%async_computation.3 | async-start | bytes 589824 | tf_op jit(solution)/shard_map/all_to_all | solution.py:313
  92.3 0.6 pad_add_fusion.place_ref
  93.0 8.7 %all-to-all-done.3.r_ref = f32[8,72,128]{2,1,0:T(8,128)S(1)} async-done(((f32[8,72,128]{2,1,0:T(8,128)}), f32[8,72,128]{2,1,0:T(8,128)S(1)}, u32[]{:S(2)}, u32[]{:S(2)}) %all-to-all-start.3) | async-done | bytes 294944 | tf_op jit(solution)/shard_map/all_to_all | solution.py:313
  101.7 0.0 copy-start.1
  101.7 0.7 copy-done.1
  102.4 1.8 %final.1 = (f32[1,1,64,1024]{3,2,1,0:T(8,128)}, f32[8,128]{1,0:T(8,128)}) custom-call(s32[2]{0:T(128)} %pad_add_fusion.place_ref, f32[8,72,128]{2,1,0:T(8,128)} %copy-done.1, f32[1,1,64,1024]{3,2,1,0:T(8,128)} %g_ref.3), custom_call_target="tpu_custom_call" | custom-call | tf_op jit(solution)/shard_map/final/pallas_call | solution.py:167
  104.2 1.3 %slice_reduce_fusion = f32[2]{0:T(128)} fusion(f32[8,128]{1,0:T(8,128)} %get-tuple-element.27), kind=kLoop, calls=%fused_computation | loop fusion | bytes 16 | tf_op jit(solution)/shard_map/slice | solution.py:318
  (1 shorter events, 0.0 us)
Async XLA Ops:
  2.2 5.9 %collective-permute-start = (f32[128,128]{1,0:T(8,128)}, f32[128,128]{1,0:T(8,128)S(1)}, u32[]{:S(2)}, u32[]{:S(2)}) collective-permute-start(f32[128,128]{1,0:T(8,128)} %get-tuple-element.15), channel_id=1, source_target_pairs={{0,1},{1,2},{2,3},{4,5},{5,6},{6,7},{8,9},{9,10},{10,11},{12,13},{... | collective-permute-start | bytes 196616 | tf_op jit(solution)/shard_map/ppermute | solution.py:272
  6.2 5.2 %collective-permute-start.1 = (f32[128,128]{1,0:T(8,128)}, f32[128,128]{1,0:T(8,128)S(1)}, u32[]{:S(2)}, u32[]{:S(2)}) collective-permute-start(f32[128,128]{1,0:T(8,128)} %get-tuple-element.16), channel_id=1, source_target_pairs={{1,0},{2,1},{3,2},{5,4},{6,5},{7,6},{9,8},{10,9},{11,10},{13,12},{... | collective-permute-start | bytes 196616 | tf_op jit(solution)/shard_map/ppermute | solution.py:273
  8.1 3.3 %copy-start.2 = (f32[128,128]{1,0:T(8,128)}, f32[128,128]{1,0:T(8,128)S(1)}, u32[]{:S(2)}) copy-start(f32[128,128]{1,0:T(8,128)S(1)} %collective-permute-done.low_ref) | copy-start | bytes 196612
  11.4 0.6 copy-start.3
  16.5 8.7 %copy-start.4 = (f32[8,128]{1,0:T(8,128)S(1)}, f32[8,128]{1,0:T(8,128)}, u32[]{:S(2)}) copy-start(f32[8,128]{1,0:T(8,128)} %get-tuple-element.18) | copy-start | bytes 12292
  16.5 20.4 %all-to-all-start = ((f32[8,96,128]{2,1,0:T(8,128)}), f32[8,96,128]{2,1,0:T(8,128)S(1)}, u32[]{:S(2)}, u32[]{:S(2)}) async-start(f32[8,96,128]{2,1,0:T(8,128)} %get-tuple-element.17), calls=%async_computation | async-start | bytes 786432 | tf_op jit(solution)/shard_map/all_to_all | solution.py:289
  25.2 4.6 %collective-permute-start.2 = (f32[8,128]{1,0:T(8,128)S(1)}, f32[8,128]{1,0:T(8,128)S(1)}, u32[]{:S(2)}, u32[]{:S(2)}) collective-permute-start(f32[8,128]{1,0:T(8,128)S(1)} %copy-done.4), channel_id=1, source_target_pairs={{0,1},{1,0},{2,3},{3,2},{4,5},{5,4},{6,7},{7,6},{8,9},{9,8},{10,11... | collective-permute-start | bytes 12296 | tf_op jit(solution)/shard_map/ppermute | solution.py:287
  29.9 5.8 %collective-permute-start.3 = (f32[8,128]{1,0:T(8,128)S(1)}, f32[8,128]{1,0:T(8,128)S(1)}, u32[]{:S(2)}, u32[]{:S(2)}) collective-permute-start(f32[8,128]{1,0:T(8,128)S(1)} %add.19), channel_id=1, source_target_pairs={{0,2},{1,3},{2,0},{3,1},{4,6},{5,7},{6,4},{7,5},{8,10},{9,11},{10,... | collective-permute-start | bytes 12296 | tf_op jit(solution)/shard_map/ppermute | solution.py:287
  36.9 0.7 copy-start
  81.1 20.6 %all-to-all-start.3 = ((f32[8,72,128]{2,1,0:T(8,128)}), f32[8,72,128]{2,1,0:T(8,128)S(1)}, u32[]{:S(2)}, u32[]{:S(2)}) async-start(f32[8,72,128]{2,1,0:T(8,128)} %back.1), calls=%async_computation.3 | async-start | bytes 589824 | tf_op jit(solution)/shard_map/all_to_all | solution.py:313
  101.7 0.7 copy-start.1

commit v2 on v1

v2 whole, which is shorter than its diff:
```python
import functools

import jax
import jax.numpy as jnp
from jax import lax
from jax.experimental import pallas as pl
from jax.experimental.pallas import tpu as pltpu
from jax.sharding import Mesh
from jax.sharding import PartitionSpec as P

WIDTH = 64
STEP = 0.0078125
TM = ("x", "zh", "zl", "c")
NEAR = ("zl", "c")
F32 = jnp.float32
BF16 = jnp.bfloat16


def split3(m):
    hi = m.astype(BF16)
    return hi, (m - hi.astype(F32)).astype(BF16)


def left3(m):
    hi, lo = split3(m)
    return jnp.concatenate([hi, hi, lo], axis=1)


def right3(v):
    hi, lo = split3(v)
    return jnp.concatenate([hi, lo, hi], axis=0)


def mix(m, v):
    return jnp.dot(left3(m), right3(v), preferred_element_type=F32)


def fold(m):
    half = m.shape[0] // 2
    return jnp.concatenate([m[:half], m[half:]], axis=1)


def unfold(m):
    half = m.shape[1] // 2
    return jnp.concatenate([m[:, :half], m[:, half:]], axis=0)


def eye(n):
    return (
        lax.broadcasted_iota(jnp.int32, (n, n), 0) == lax.broadcasted_iota(jnp.int32, (n, n), 1)
    ).astype(F32)


def edge_kernel(g_ref, p_ref, up_ref, down_ref, p_first, p_last, sems):
    end = g_ref.shape[3] - 128
    copies = [
        pltpu.make_async_copy(p_ref.at[:, 0, :, pl.ds(0, 128)], p_first, sems.at[0]),
        pltpu.make_async_copy(p_ref.at[:, 0, :, pl.ds(end, 128)], p_last, sems.at[1]),
        pltpu.make_async_copy(g_ref.at[0, 0, :, pl.ds(0, 128)], up_ref.at[pl.ds(0, 64)], sems.at[2]),
        pltpu.make_async_copy(
            g_ref.at[0, 0, :, pl.ds(end, 128)], down_ref.at[pl.ds(0, 64)], sems.at[3]
        ),
    ]
    for copy in copies:
        copy.start()
    for copy in copies[:2]:
        copy.wait()
    up_ref[64:] = jnp.concatenate([p_first[n].astype(F32)[:, :WIDTH] for n in range(2)], axis=1)
    down_ref[64:] = jnp.concatenate([p_last[n].astype(F32)[:, WIDTH:] for n in range(2)], axis=1)
    for copy in copies[2:]:
        copy.wait()


def edges(guess, probes):
    return pl.pallas_call(
        edge_kernel,
        in_specs=[pl.BlockSpec(memory_space=pltpu.HBM)] * 2,
        out_specs=[whole()] * 2,
        out_shape=[jax.ShapeDtypeStruct((128, 128), F32)] * 2,
        scratch_shapes=[pltpu.VMEM((2, 64, 128), BF16)] * 2 + [pltpu.SemaphoreType.DMA((4,))],
        compiler_params=pltpu.CompilerParams(vmem_limit_bytes=(64 << 20) - (256 << 10)),
        name="edges",
    )(guess, probes)


def taps(v):
    n = v.shape[1]
    column = lax.broadcasted_iota(jnp.int32, v.shape, 1) & (WIDTH - 1)
    left = pltpu.roll(jnp.where(column == WIDTH - 1, 0.0, v), 1, 1)
    right = pltpu.roll(jnp.where(column == 0, 0.0, v), n - 1, 1)
    rows = []
    for part in (left, v, right):
        above = pltpu.roll(part, WIDTH, 1)
        below = jnp.concatenate([above[:, 128:], above[:, :128]], axis=1)
        rows.append((above, part, below))
    return jnp.concatenate(
        [rows[dx][dy].astype(BF16) for dy in range(3) for dx in range(3)], axis=0
    )


def rounded(v):
    return v.astype(BF16).astype(F32)


def convolve(kernel, v, at=None):
    stack = taps(rounded(v))
    return jnp.dot(kernel, stack if at is None else stack[:, at], preferred_element_type=F32)


def bias_of(b_ref, layer):
    return jnp.sum(
        jnp.where(eye(64) == 1.0, b_ref[layer : layer + 1, :], 0.0), axis=1, keepdims=True
    )


def side(ref, n):
    return ref[64:, n * WIDTH : (n + 1) * WIDTH]


def inner_kernel(place_ref, g_ref, p_ref, k_ref, b_ref, state_ref, offset_ref, change_ref, t_ref):
    leading = place_ref[0] == 0
    g = g_ref[0, 0]
    cells = g.shape[1]
    kernel = k_ref[0]
    activation = jnp.tanh(g)
    slopes = 1.0 - activation * activation
    forcing = STEP * (convolve(kernel, activation) + bias_of(b_ref, 0))
    total = jnp.zeros((64, cells), F32)
    for n in range(2):
        probe = p_ref[n, 0].astype(F32)
        total = total + probe * convolve(kernel, slopes * probe)
    lane = lax.broadcasted_iota(jnp.int32, (64, cells), 1)
    total = jnp.where((lane >= WIDTH) & (lane < cells - WIDTH), total, 0.0)
    t_ref[...] = jnp.full((8, 128), 0.5 * jnp.sum(total))
    both = k_ref[0].astype(F32) + k_ref[1].astype(F32)
    pair = both[:, :128] + both[:, 128:256] + both[:, 256:384] + both[:, 384:512]
    coarse = STEP * (pair[:, :64] + pair[:, 64:] + both[:, 512:])
    state_ref[...] = g + forcing
    offset_ref[...] = forcing + jnp.where(leading, g, -mix(coarse, g))
    change_ref[...] = fold(jnp.where(leading, -eye(64), coarse))


def outer_kernel(
    strips,
    strip_ref,
    g_ref,
    low_ref,
    high_ref,
    p_ref,
    k_ref,
    b_ref,
    state_ref,
    offset_ref,
    change_ref,
    inner_ref,
    send_ref,
    t_ref,
):
    cells = state_ref.shape[1]
    last = cells - 128
    zero = jnp.zeros((64, WIDTH), F32)
    ends = jnp.concatenate(
        [low_ref[:64], g_ref[0, 0, :, :128], g_ref[0, 0, :, last:], high_ref[:64]], axis=1
    )
    probe_mid = [p_ref[n, 0].astype(F32) for n in range(2)]
    activation = jnp.tanh(ends)
    slopes = 1.0 - activation * activation
    kernel = k_ref[0]
    forcing = STEP * (convolve(kernel, activation) + bias_of(b_ref, 0))
    total = jnp.zeros((64, 128), F32)
    for n in range(2):
        probe = jnp.concatenate(
            [
                zero,
                side(low_ref, n),
                probe_mid[n][:, :128],
                probe_mid[n][:, last:],
                side(high_ref, n),
                zero,
            ],
            axis=1,
        )
        found = convolve(kernel, slopes * probe, slice(128, 384))
        total = total + jnp.concatenate(
            [
                probe_mid[n][:, :WIDTH] * found[:, :WIDTH],
                probe_mid[n][:, last + WIDTH :] * found[:, 256 - WIDTH :],
            ],
            axis=1,
        )
    rows = lax.broadcasted_iota(jnp.int32, (8, 128), 0)
    trace = inner_ref[...] + 0.5 * jnp.sum(total)

    lane = lax.broadcasted_iota(jnp.int32, (64, 128), 1)
    fresh = ends + forcing
    first, final = state_ref[:, :128], state_ref[:, last:]
    new_first = jnp.where(lane < WIDTH, fresh[:, 128:256], first)
    new_final = jnp.where(lane < WIDTH, final, fresh[:, 256:384])
    current = jnp.concatenate(
        [fresh[:, :128], new_first, state_ref[:, 128:last], new_final, fresh[:, 384:]], axis=1
    )
    wide = cells + 256
    far_lane = lax.broadcasted_iota(jnp.int32, (64, wide), 1)
    outside = ((strip_ref[0] == 0) & (far_lane < 128)) | (
        (strip_ref[0] == strips - 1) & (far_lane >= wide - 128)
    )
    middle = slice(128, 128 + cells)
    activation = jnp.where(outside, 0.0, jnp.tanh(current))
    slopes = 1.0 - activation * activation
    kernel = k_ref[1]
    forcing = STEP * (convolve(kernel, activation, middle) + bias_of(b_ref, 1))
    total = jnp.zeros((64, cells), F32)
    for n in range(2):
        probe = jnp.concatenate(
            [zero, side(low_ref, n), probe_mid[n], side(high_ref, n), zero], axis=1
        )
        total = total + probe_mid[n] * convolve(kernel, slopes * probe, middle)
    trace = jnp.where(rows == 1, 0.5 * jnp.sum(total), jnp.where(rows == 0, trace, 0.0))
    t_ref[...] = trace
    for j in range(cells // 128):
        at = slice(j * 128, (j + 1) * 128)
        part = offset_ref[:, at] + forcing[:, at]
        if j == 0:
            part = part + (new_first - first)
        if j == cells // 128 - 1:
            part = part + (new_final - final)
        send_ref[j, :64] = part
        send_ref[j, 64:] = change_ref[...]


def whole(*shape):
    return pl.BlockSpec(memory_space=pltpu.VMEM)


def scalars():
    return pl.BlockSpec(memory_space=pltpu.SMEM)


def call(kernel, shapes, places, args, name, room, cost=None):
    return pl.pallas_call(
        kernel,
        in_specs=[scalars()] * places + [whole()] * (len(args) - places),
        out_specs=[whole() if len(s) > 1 else scalars() for s in shapes],
        out_shape=[jax.ShapeDtypeStruct(s, F32) for s in shapes],
        compiler_params=pltpu.CompilerParams(vmem_limit_bytes=room << 20),
        cost_estimate=cost,
        name=name,
    )(*args)


def advance(matrix, value, change, offset):
    wide = jnp.concatenate([value, matrix], axis=1)
    moved = wide + mix(change, wide)
    return moved[:, 128:], moved[:, :128] + offset


def join(earlier, later):
    change, offset = later
    wide = jnp.concatenate([earlier[1], earlier[0]], axis=1)
    moved = wide + mix(change, wide)
    return moved[:, 128:] + change, moved[:, :128] + offset


def near_kernel(r_ref, *refs):
    traces, (send_ref, value_ref, matrix_ref) = refs[:-3], refs[-3:]
    count = r_ref.shape[0]
    spans = [(unfold(r_ref[j, 64:96]), r_ref[j, :64]) for j in range(count)]
    before = [None] + spans[:1]
    pairs = [join(spans[j], spans[j + 1]) for j in range(0, count, 2)]
    upto = pairs[:1]
    if count == 8:
        quads = [join(pairs[0], pairs[1]), join(pairs[2], pairs[3])]
        total = join(quads[0], quads[1])
        upto = [pairs[0], quads[0], join(quads[0], pairs[2])]
    else:
        total = join(pairs[0], pairs[1])
    for i, span in enumerate(upto):
        before += [span, join(span, spans[2 * i + 2])]
    for j in range(count):
        matrix, value = before[j] if j else (jnp.zeros((64, 64), F32), jnp.zeros((64, 128), F32))
        value_ref[j] = value
        matrix_ref[j] = matrix
    change, value = fold(total[0]), total[1]
    trace = sum(t[...] for t in traces)
    for i in range(send_ref.shape[0]):
        send_ref[i, :64] = value
        send_ref[i, 64:96] = change
        send_ref[i, 96:] = trace


def far_kernel(place_ref, r_ref, send_ref, value_ref, matrix_ref, t_ref):
    count = r_ref.shape[0]
    me = place_ref[0]
    rows = lax.broadcasted_iota(jnp.int32, (8, 128), 0)
    matrix, value = eye(64), jnp.zeros((64, 128), F32)
    own_matrix, own_value = matrix, value
    before = total = own = jnp.zeros((8, 128), F32)
    for i in range(count):
        own_matrix = jnp.where(me == i, matrix, own_matrix)
        own_value = jnp.where(me == i, value, own_value)
        t = r_ref[i, 96:]
        before = jnp.where(me == i, total, before)
        own = jnp.where(me == i, t, own)
        total = total + t
        matrix, value = advance(matrix, value, unfold(r_ref[i, 64:96]), r_ref[i, :64])
    value_ref[...] = own_value
    matrix_ref[...] = own_matrix
    spread = jnp.sum(before, axis=0, keepdims=True)
    t_ref[...] = jnp.where(rows == 2, spread, own)
    change = fold(matrix - eye(64))
    for i in range(send_ref.shape[0]):
        send_ref[i, :64] = value
        send_ref[i, 64:96] = change
        send_ref[i, 96:] = total


def back_kernel(place_ref, r_ref, far_value, far_matrix, t_ref, near_value, near_matrix, send_ref):
    me = place_ref[0]
    rows = lax.broadcasted_iota(jnp.int32, (8, 128), 0)
    state = own = jnp.zeros((64, 128), F32)
    before = total = jnp.zeros((8, 128), F32)
    count = r_ref.shape[0]
    for i in range(count):
        own = jnp.where(me == i, state, own)
        before = jnp.where(me == i, total, before)
        total = total + r_ref[i, 96:]
        if i < count - 1:
            state = state + mix(unfold(r_ref[i, 64:96]), state) + r_ref[i, :64]
    entry = mix(far_matrix[...], own) + far_value[...]
    near = near_matrix.shape[0]
    states = mix(near_matrix[...].reshape(near * 64, 64), entry)
    spread = jnp.sum(before, axis=0, keepdims=True)
    t = t_ref[...] + jnp.where(rows == 2, spread, 0.0)
    for j in range(near):
        send_ref[j, :64] = entry + states[j * 64 : (j + 1) * 64] + near_value[j]
        send_ref[j, 64:] = t


def final_kernel(place_ref, me_ref, r_ref, g_ref, state_ref, log_ref):
    leading, me = place_ref[0] == 0, me_ref[0]
    count = r_ref.shape[0]
    earlier = jnp.zeros((1, 128), F32)
    own = jnp.zeros((8, 128), F32)
    for j in range(count):
        at = slice(j * 128, (j + 1) * 128)
        state_ref[0, 0, :, at] = jnp.where(leading, g_ref[0, 0, :, at], r_ref[j, :64])
        t = r_ref[j, 64:]
        earlier = earlier + t[2:3] + jnp.where(j < me, t[0:1] + t[1:2], 0.0)
        own = jnp.where(me == j, t, own)
    first = earlier + own[0:1]
    second = first + own[1:2]
    log_ref[0] = -(STEP / WIDTH) * first[0, 0]
    log_ref[1] = -(STEP / WIDTH) * second[0, 0]


def body(guess, kernels, biases, probes):
    strips = lax.axis_size("space")
    strip = lax.axis_index("space")
    near = lax.axis_size("zl") * lax.axis_size("c")
    far, last = lax.axis_size("zh"), lax.axis_size("x")
    cells = guess.shape[3]
    place = lax.axis_index(TM).reshape(1)

    up, down = edges(guess, probes)
    forward = [(i, i + 1) for i in range(strips - 1)]
    backward = [(i + 1, i) for i in range(strips - 1)]
    low = lax.ppermute(down, "space", forward)
    high = lax.ppermute(up, "space", backward)
    state, offset, change, inner = call(
        inner_kernel,
        [(64, cells), (64, cells), (32, 128), (8, 128)],
        1,
        (place, guess, probes, kernels, biases),
        "inner",
        20,
        pl.CostEstimate(flops=450_000_000, bytes_accessed=2_000_000, transcendentals=65536),
    )
    send, trace = call(
        functools.partial(outer_kernel, strips),
        [(near, 96, 128), (8, 128)],
        1,
        (
            strip.reshape(1), guess, low, high, probes, kernels, biases,
            state, offset, change, inner,
        ),
        "outer",
        20,
    )
    got = lax.all_to_all(send, NEAR, 0, 0, tiled=True)
    traces = [
        lax.ppermute(trace, "space", [(i, (i + hop) % strips) for i in range(strips)])
        for hop in range(1, strips)
    ]
    send, near_value, near_matrix = call(
        near_kernel,
        [(far, 104, 128), (near, 64, 128), (near, 64, 64)],
        0,
        (got, trace, *traces),
        "near",
        8,
    )
    got = lax.all_to_all(send, "zh", 0, 0, tiled=True)
    send, far_value, far_matrix, trace = call(
        far_kernel,
        [(last, 104, 128), (64, 128), (64, 64), (8, 128)],
        1,
        (lax.axis_index("zh").reshape(1), got),
        "far",
        8,
    )
    got = lax.all_to_all(send, "x", 0, 0, tiled=True)
    (send,) = call(
        back_kernel,
        [(near, 72, 128)],
        1,
        (lax.axis_index("x").reshape(1), got, far_value, far_matrix, trace, near_value, near_matrix),
        "back",
        8,
    )
    got = lax.all_to_all(send, NEAR, 0, 0, tiled=True)
    return call(
        final_kernel,
        [(1, 1, 64, cells), (2,)],
        2,
        (place, lax.axis_index(NEAR).reshape(1), got, guess),
        "final",
        8,
    )


def solution(mesh):
    finer = Mesh(
        mesh.devices.reshape(4, 4, 4, 2, mesh.shape["space"]), ("x", "zh", "zl", "c", "space")
    )
    placed = (
        P(TM, None, None, "space"),
        P(TM, None, None),
        P(TM, None),
        P(None, None, None, "space"),
    )
    return jax.shard_map(
        body,
        mesh=finer,
        in_specs=placed,
        out_specs=(P(TM, None, None, "space"), P(TM)),
        check_vma=False,
    )
```

time: 106 us -> 95.5 us (0.901)
  blocking collectives: 35.2 us -> 56.3 us
  waiting for transfers between devices: 16.5 us -> 3.57 us
  starting transfers between devices: 31.8 us -> 22.7 us
  Pallas kernels: 16 us -> 9.13 us
  other arithmetic: 1.81 us -> 0 us
    all_to_all x0 -> x1, blocking collectives: none -> 21.5 us  [body(): got = lax.all_to_all(send, NEAR, 0, 0, tiled=True)]
    all_to_all x2 -> x1, starting transfers between devices: 20 us -> 8.42 us  [body(): got = lax.all_to_all(send, NEAR, 0, 0, tiled=True)]
    all_to_all x2 -> x1, waiting for transfers between devices: 9.26 us -> 0.01 us  [body(): got = lax.all_to_all(send, NEAR, 0, 0, tiled=True)]
    pallas_call x5 -> x6, Pallas kernels: 14.5 us -> 7.56 us  [call(): pl.pallas_call(kernel, in_specs=[scalars()] * places + [whole()] * (len(a...]
    ppermute x1, waiting for transfers between devices: 3.3 us -> 0.01 us  [body(): high = lax.ppermute(up, 'space', backward)]
    ppermute x2 -> x3, starting transfers between devices: 6.5 us -> 8.98 us  [body(): lax.ppermute(trace, 'space', [(i, (i + hop) % strips) for i in range(stri...]
    slice x1 -> x0, local copies, waits for them, and re-layouts: 1.31 us -> none  [body(): return (states, log_change[:2, 0])]
    another operation x2 -> x0, other arithmetic: 1.21 us -> none  [the longest x1 0.62 us: body(): place = jnp.stack([leading, lax.axis_index(NEAR)])]
  transfers between devices with their start and end apart: 6 -> 6, of which waited for: 5 -> 2; matrix products, arithmetic and copies ran while one was open for 2% -> 0% of each run, Pallas kernels for 0% -> 2%
where the time goes in v2:
time: 95.5 us; the launch traced here: 95 us
  blocking collectives  56.3 us (59%)
  starting transfers between devices  22.7 us (24%)
  Pallas kernels  9.13 us (10%)
  waiting for transfers between devices  3.57 us (4%)
  local copies, waits for them, and re-layouts  2.57 us (3%)
    all_to_all x1, blocking collectives, body(): got = lax.all_to_all(send, 'zh', 0, 0, tiled=True)  25.7 us
    all_to_all x1, blocking collectives, body(): got = lax.all_to_all(send, NEAR, 0, 0, tiled=True)  21.5 us
    all_to_all x1, blocking collectives, body(): got = lax.all_to_all(send, 'x', 0, 0, tiled=True)  9.07 us
    ppermute x3, starting transfers between devices, body(): lax.ppermute(trace, 'space', [(i, (i + hop) % strips) for i in range(stri...  8.98 us
    all_to_all x1, starting transfers between devices, body(): got = lax.all_to_all(send, NEAR, 0, 0, tiled=True)  8.42 us
    pallas_call x6, Pallas kernels, call(): pl.pallas_call(kernel, in_specs=[scalars()] * places + [whole()] * (len(a...  7.56 us
    ppermute x1, starting transfers between devices, body(): low = lax.ppermute(down, 'space', forward)  4.02 us
    ppermute x3, waiting for transfers between devices, body(): lax.ppermute(trace, 'space', [(i, (i + hop) % strips) for i in range(stri...  3.56 us
  transfers between devices with their start and end apart: 6, of which 2 were waited for; matrix products, arithmetic and copies ran while one was open for 0% of the time, Pallas kernels for 2%

profile of v2, /device:TPU:1, one launch (start us, length us, event | category | flops | bytes accessed | tf_op | source)
XLA Modules:
  0.0 95.0 jit_solution(17442720405689037132)
XLA Ops:
  0.6 0.0 copy-start.3
  0.6 1.6 %edges.1 = (f32[128,128]{1,0:T(8,128)}, f32[128,128]{1,0:T(8,128)}) custom-call(f32[1,1,64,1024]{3,2,1,0:T(8,128)} %g_ref.7, bf16[2,1,64,1024]{3,2,1,0:T(8,128)(2,1)} %p_ref.5), custom_call_target="tpu_custom_call" | custom-call | tf_op jit(solution)/shard_map/edges/pallas_call | solution.py:75
  2.2 4.0 %collective-permute-start = (f32[128,128]{1,0:T(8,128)}, f32[128,128]{1,0:T(8,128)S(1)}, u32[]{:S(2)}, u32[]{:S(2)}) collective-permute-start(f32[128,128]{1,0:T(8,128)} %get-tuple-element.17), channel_id=1, source_target_pairs={{0,1},{1,2},{2,3},{4,5},{5,6},{6,7},{8,9},{9,10},{10,11},{12,13},{... | collective-permute-start | bytes 196616 | tf_op jit(solution)/shard_map/ppermute | solution.py:367
  6.2 1.3 %collective-permute-start.1 = (f32[128,128]{1,0:T(8,128)}, f32[128,128]{1,0:T(8,128)S(1)}, u32[]{:S(2)}, u32[]{:S(2)}) collective-permute-start(f32[128,128]{1,0:T(8,128)} %get-tuple-element.18), channel_id=1, source_target_pairs={{1,0},{2,1},{3,2},{5,4},{6,5},{7,6},{9,8},{10,9},{11,10},{13,12},{... | collective-permute-start | bytes 196616 | tf_op jit(solution)/shard_map/ppermute | solution.py:368
  7.6 0.0 copy-start.4
  7.6 0.0 copy-done.3
  7.6 0.7 copy-done.4
  8.2 0.0 copy-start
  8.2 0.9 copy-done
  9.2 0.0 copy-start.2
  9.2 0.9 copy-done.2
  10.1 1.5 %inner.1 = (f32[64,1024]{1,0:T(8,128)S(1)}, f32[64,1024]{1,0:T(8,128)S(1)}, f32[32,128]{1,0:T(8,128)S(1)}, f32[8,128]{1,0:T(8,128)S(1)}) custom-call(s32[1]{0:T(128)} %bitcast.place_ref, f32[1,1,64,1024]{3,2,1,0:T(8,128)S(1)} %copy-done, bf16[2,1,64,1024]{3,2,1,0:T(8,128)(2,1)S(1)} %copy-done.2, bf16[2,64,576]{2,1,0:T(8,128)(2,1)S(1)} %copy-done.3, ...), custom_call_target="tpu_custom_call" | custom-call | flops 450000000 | bytes 2000000 | tf_op jit(solution)/shard_map/inner/pallas_call | solution.py:240
  11.6 0.0 collective-permute-done.low_ref
  11.6 0.0 collective-permute-done.1.high_ref
  11.7 2.8 %outer.1 = (f32[8,96,128]{2,1,0:T(8,128)}, f32[8,128]{1,0:T(8,128)S(1)}) custom-call(s32[1]{0:T(128)} %bitcast.4.strip_ref, f32[1,1,64,1024]{3,2,1,0:T(8,128)S(1)} %copy-done, f32[128,128]{1,0:T(8,128)S(1)} %collective-permute-done.low_ref, f32[128,128]{1,0:T(8,128)S(1)} %collective-permute-done.1.high_ref, bf16[2,1,64,1024]{3,2,1,0:T(8,128)(2,1)S(1)} %copy-done.2, ...), custom_call_target="tpu_custom_call" | custom-call | tf_op jit(solution)/shard_map/outer/pallas_call | solution.py:240
  14.5 8.4 %all-to-all-start = ((f32[8,96,128]{2,1,0:T(8,128)}), f32[8,96,128]{2,1,0:T(8,128)S(1)}, u32[]{:S(2)}, u32[]{:S(2)}) async-start(f32[8,96,128]{2,1,0:T(8,128)} %get-tuple-element.23), calls=%async_computation | async-start | bytes 786432 | tf_op jit(solution)/shard_map/all_to_all | solution.py:389
  22.9 4.1 %collective-permute-start.4 = (f32[8,128]{1,0:T(8,128)S(1)}, f32[8,128]{1,0:T(8,128)S(1)}, u32[]{:S(2)}, u32[]{:S(2)}) collective-permute-start(f32[8,128]{1,0:T(8,128)S(1)} %get-tuple-element.24.refs_0_), channel_id=1, source_target_pairs={{0,3},{1,0},{2,1},{3,2},{4,7},{5,4},{6,5},{7,6},{8,11},{9,8},{10,9... | collective-permute-start | bytes 12296 | tf_op jit(solution)/shard_map/ppermute | solution.py:391
  27.1 2.9 %collective-permute-start.3 = (f32[8,128]{1,0:T(8,128)S(1)}, f32[8,128]{1,0:T(8,128)S(1)}, u32[]{:S(2)}, u32[]{:S(2)}) collective-permute-start(f32[8,128]{1,0:T(8,128)S(1)} %get-tuple-element.24.refs_0_), channel_id=1, source_target_pairs={{0,2},{1,3},{2,0},{3,1},{4,6},{5,7},{6,4},{7,5},{8,10},{9,11},{10,... | collective-permute-start | bytes 12296 | tf_op jit(solution)/shard_map/ppermute | solution.py:391
  29.9 2.0 %collective-permute-start.2 = (f32[8,128]{1,0:T(8,128)S(1)}, f32[8,128]{1,0:T(8,128)S(1)}, u32[]{:S(2)}, u32[]{:S(2)}) collective-permute-start(f32[8,128]{1,0:T(8,128)S(1)} %get-tuple-element.24.refs_0_), channel_id=1, source_target_pairs={{0,1},{1,2},{2,3},{3,0},{4,5},{5,6},{6,7},{7,4},{8,9},{9,10},{10,1... | collective-permute-start | bytes 12296 | tf_op jit(solution)/shard_map/ppermute | solution.py:391
  31.9 0.0 collective-permute-done.4.refs_3_
  31.9 1.0 %collective-permute-done.3.refs_2_ = f32[8,128]{1,0:T(8,128)S(1)} collective-permute-done((f32[8,128]{1,0:T(8,128)S(1)}, f32[8,128]{1,0:T(8,128)S(1)}, u32[]{:S(2)}, u32[]{:S(2)}) %collective-permute-start.3) | collective-permute-done | bytes 4128 | tf_op jit(solution)/shard_map/ppermute | solution.py:391
  32.9 2.6 %collective-permute-done.2.refs_1_ = f32[8,128]{1,0:T(8,128)S(1)} collective-permute-done((f32[8,128]{1,0:T(8,128)S(1)}, f32[8,128]{1,0:T(8,128)S(1)}, u32[]{:S(2)}, u32[]{:S(2)}) %collective-permute-start.2) | collective-permute-done | bytes 4128 | tf_op jit(solution)/shard_map/ppermute | solution.py:391
  35.5 0.0 all-to-all-done.r_ref
  35.5 0.8 near.1
  36.3 25.7 %all_to_all.20.r_ref = f32[4,104,128]{2,1,0:T(8,128)S(1)} all-to-all(f32[4,104,128]{2,1,0:T(8,128)S(1)} %get-tuple-element.25), channel_id=1, replica_groups=mesh['x'=4,'zh'=4,'zl'=4,'c'=2,'space'=4] {'zh'}, dimensions={0} | all-to-all | bytes 425984 | tf_op jit(solution)/shard_map/all_to_all | solution.py:402
  62.0 0.8 far.1
  62.8 9.1 %all_to_all.21.r_ref = f32[4,104,128]{2,1,0:T(8,128)S(1)} all-to-all(f32[4,104,128]{2,1,0:T(8,128)S(1)} %get-tuple-element.26), channel_id=1, replica_groups=mesh['x'=4,'zh'=4,'zl'=4,'c'=2,'space'=4] {'x'}, dimensions={0} | all-to-all | bytes 425984 | tf_op jit(solution)/shard_map/all_to_all | solution.py:411
  71.8 0.9 back.1
  72.8 0.0 copy-start.1
  72.8 21.5 %all_to_all.22.r_ref = f32[8,72,128]{2,1,0:T(8,128)S(1)} all-to-all(f32[8,72,128]{2,1,0:T(8,128)S(1)} %back.1), channel_id=1, replica_groups=mesh['x'=4,'zh'=4,'zl'=4,'c'=2,'space'=4] {'zl','c'}, dimensions={0} | all-to-all | bytes 589824 | tf_op jit(solution)/shard_map/all_to_all | solution.py:420
  94.3 0.0 copy-done.1
  94.3 0.7 final.1
Async XLA Ops:
  0.6 6.9 %copy-start.3 = (bf16[2,64,576]{2,1,0:T(8,128)(2,1)S(1)}, bf16[2,64,576]{2,1,0:T(8,128)(2,1)}, u32[]{:S(2)}) copy-start(bf16[2,64,576]{2,1,0:T(8,128)(2,1)} %k_ref.3) | copy-start | bytes 442372
  2.2 9.4 %collective-permute-start = (f32[128,128]{1,0:T(8,128)}, f32[128,128]{1,0:T(8,128)S(1)}, u32[]{:S(2)}, u32[]{:S(2)}) collective-permute-start(f32[128,128]{1,0:T(8,128)} %get-tuple-element.17), channel_id=1, source_target_pairs={{0,1},{1,2},{2,3},{4,5},{5,6},{6,7},{8,9},{9,10},{10,11},{12,13},{... | collective-permute-start | bytes 196616 | tf_op jit(solution)/shard_map/ppermute | solution.py:367
  6.2 5.4 %collective-permute-start.1 = (f32[128,128]{1,0:T(8,128)}, f32[128,128]{1,0:T(8,128)S(1)}, u32[]{:S(2)}, u32[]{:S(2)}) collective-permute-start(f32[128,128]{1,0:T(8,128)} %get-tuple-element.18), channel_id=1, source_target_pairs={{1,0},{2,1},{3,2},{5,4},{6,5},{7,6},{9,8},{10,9},{11,10},{13,12},{... | collective-permute-start | bytes 196616 | tf_op jit(solution)/shard_map/ppermute | solution.py:368
  7.6 0.7 copy-start.4
  8.2 0.9 copy-start
  9.2 0.9 copy-start.2
  14.5 21.0 %all-to-all-start = ((f32[8,96,128]{2,1,0:T(8,128)}), f32[8,96,128]{2,1,0:T(8,128)S(1)}, u32[]{:S(2)}, u32[]{:S(2)}) async-start(f32[8,96,128]{2,1,0:T(8,128)} %get-tuple-element.23), calls=%async_computation | async-start | bytes 786432 | tf_op jit(solution)/shard_map/all_to_all | solution.py:389
  22.9 9.0 %collective-permute-start.4 = (f32[8,128]{1,0:T(8,128)S(1)}, f32[8,128]{1,0:T(8,128)S(1)}, u32[]{:S(2)}, u32[]{:S(2)}) collective-permute-start(f32[8,128]{1,0:T(8,128)S(1)} %get-tuple-element.24.refs_0_), channel_id=1, source_target_pairs={{0,3},{1,0},{2,1},{3,2},{4,7},{5,4},{6,5},{7,6},{8,11},{9,8},{10,9... | collective-permute-start | bytes 12296 | tf_op jit(solution)/shard_map/ppermute | solution.py:391
  27.1 5.9 %collective-permute-start.3 = (f32[8,128]{1,0:T(8,128)S(1)}, f32[8,128]{1,0:T(8,128)S(1)}, u32[]{:S(2)}, u32[]{:S(2)}) collective-permute-start(f32[8,128]{1,0:T(8,128)S(1)} %get-tuple-element.24.refs_0_), channel_id=1, source_target_pairs={{0,2},{1,3},{2,0},{3,1},{4,6},{5,7},{6,4},{7,5},{8,10},{9,11},{10,... | collective-permute-start | bytes 12296 | tf_op jit(solution)/shard_map/ppermute | solution.py:391
  29.9 5.6 %collective-permute-start.2 = (f32[8,128]{1,0:T(8,128)S(1)}, f32[8,128]{1,0:T(8,128)S(1)}, u32[]{:S(2)}, u32[]{:S(2)}) collective-permute-start(f32[8,128]{1,0:T(8,128)S(1)} %get-tuple-element.24.refs_0_), channel_id=1, source_target_pairs={{0,1},{1,2},{2,3},{3,0},{4,5},{5,6},{6,7},{7,4},{8,9},{9,10},{10,1... | collective-permute-start | bytes 12296 | tf_op jit(solution)/shard_map/ppermute | solution.py:391
  72.8 21.5 %copy-start.1 = (f32[1,1,64,1024]{3,2,1,0:T(8,128)S(1)}, f32[1,1,64,1024]{3,2,1,0:T(8,128)}, u32[]{:S(2)}) copy-start(f32[1,1,64,1024]{3,2,1,0:T(8,128)} %g_ref.7) | copy-start | bytes 786436

commit v3 on v2

--- a/solution.py
+++ b/solution.py
@@ -12,6 +12,10 @@
 STEP = 0.0078125
 TM = ("x", "zh", "zl", "c")
 NEAR = ("zl", "c")
+SPACE = ("sh", "sl")
+VALUE_SCALE = 2048.0
+CHANGE_SCALE = 32768.0
+F16 = jnp.float16
 F32 = jnp.float32
 BF16 = jnp.bfloat16
 
@@ -51,36 +55,36 @@
     ).astype(F32)
 
 
-def edge_kernel(g_ref, p_ref, up_ref, down_ref, p_first, p_last, sems):
+def edge_kernel(g_ref, p_ref, up_ref, down_ref, gv_ref, pv_ref, sems):
     end = g_ref.shape[3] - 128
     copies = [
-        pltpu.make_async_copy(p_ref.at[:, 0, :, pl.ds(0, 128)], p_first, sems.at[0]),
-        pltpu.make_async_copy(p_ref.at[:, 0, :, pl.ds(end, 128)], p_last, sems.at[1]),
-        pltpu.make_async_copy(g_ref.at[0, 0, :, pl.ds(0, 128)], up_ref.at[pl.ds(0, 64)], sems.at[2]),
-        pltpu.make_async_copy(
-            g_ref.at[0, 0, :, pl.ds(end, 128)], down_ref.at[pl.ds(0, 64)], sems.at[3]
-        ),
+        pltpu.make_async_copy(p_ref, pv_ref, sems.at[0]),
+        pltpu.make_async_copy(g_ref, gv_ref, sems.at[1]),
     ]
     for copy in copies:
         copy.start()
-    for copy in copies[:2]:
-        copy.wait()
-    up_ref[64:] = jnp.concatenate([p_first[n].astype(F32)[:, :WIDTH] for n in range(2)], axis=1)
-    down_ref[64:] = jnp.concatenate([p_last[n].astype(F32)[:, WIDTH:] for n in range(2)], axis=1)
-    for copy in copies[2:]:
-        copy.wait()
+    copies[0].wait()
+    first = [pv_ref[n, 0, :, :WIDTH].astype(F32) for n in range(2)]
+    last = [pv_ref[n, 0, :, end + WIDTH :].astype(F32) for n in range(2)]
+    up_ref[64:] = jnp.concatenate(first, axis=1)
+    down_ref[64:] = jnp.concatenate(last, axis=1)
+    copies[1].wait()
+    up_ref[:64] = gv_ref[0, 0, :, :128]
+    down_ref[:64] = gv_ref[0, 0, :, end:]
 
 
 def edges(guess, probes):
+    held = [pltpu.with_memory_space_constraint(v, pltpu.HBM) for v in (guess, probes)]
     return pl.pallas_call(
         edge_kernel,
         in_specs=[pl.BlockSpec(memory_space=pltpu.HBM)] * 2,
-        out_specs=[whole()] * 2,
-        out_shape=[jax.ShapeDtypeStruct((128, 128), F32)] * 2,
-        scratch_shapes=[pltpu.VMEM((2, 64, 128), BF16)] * 2 + [pltpu.SemaphoreType.DMA((4,))],
-        compiler_params=pltpu.CompilerParams(vmem_limit_bytes=(64 << 20) - (256 << 10)),
+        out_specs=[whole()] * 4,
+        out_shape=[jax.ShapeDtypeStruct((128, 128), F32)] * 2
+        + [jax.ShapeDtypeStruct(guess.shape, F32), jax.ShapeDtypeStruct(probes.shape, BF16)],
+        scratch_shapes=[pltpu.SemaphoreType.DMA((2,))],
+        compiler_params=pltpu.CompilerParams(vmem_limit_bytes=4 << 20),
         name="edges",
-    )(guess, probes)
+    )(*held)
 
 
 def taps(v):
@@ -224,8 +228,8 @@
             part = part + (new_first - first)
         if j == cells // 128 - 1:
             part = part + (new_final - final)
-        send_ref[j, :64] = part
-        send_ref[j, 64:] = change_ref[...]
+        send_ref[j, :64] = VALUE_SCALE * part
+        send_ref[j, 64:] = CHANGE_SCALE * change_ref[...]
 
 
 def whole(*shape):
@@ -248,10 +252,52 @@
     )(*args)
 
 
-def advance(matrix, value, change, offset):
-    wide = jnp.concatenate([value, matrix], axis=1)
-    moved = wide + mix(change, wide)
-    return moved[:, 128:], moved[:, :128] + offset
+def exponent(v):
+    return jnp.ceil(jnp.log2(jnp.maximum(v, 1e-30)))
+
+
+def block_exponent(v):
+    return exponent(jnp.max(jnp.abs(v), axis=(0, 1), keepdims=True))
+
+
+def scaled(v, power):
+    return v * jnp.exp2(15.0 - power)
+
+
+def restored(v, power):
+    return v * jnp.exp2(power - 15.0)
+
+
+def tags(t, value_power, change_power):
+    lane = lax.broadcasted_iota(jnp.int32, (8, 128), 1)
+    power = exponent(jnp.abs(t))
+    unit = t * jnp.exp2(-power)
+    coarse = rounded(unit)
+    fine = 256.0 * (unit - coarse)
+    top = jnp.where(lane < 64, coarse, power)
+    low = jnp.where(lane < 64, fine, jnp.where(lane < 96, value_power, change_power))
+    return jnp.concatenate([top, low], axis=0)
+
+
+def read_tags(r):
+    t = (r[:8, :1] + r[8:, :1] / 256.0) * jnp.exp2(r[:8, 64:65])
+    return t, r[8:9, 64:65], r[8:9, 96:97]
+
+
+def put(ref, change, value, t):
+    value_power, change_power = block_exponent(value), block_exponent(change)
+    value = scaled(value, value_power)
+    change = scaled(fold(change), change_power)
+    extra = tags(t, value_power, change_power)
+    for i in range(ref.shape[0]):
+        ref[i, :64] = value
+        ref[i, 64:96] = change
+        ref[i, 96:] = extra
+
+
+def take(r):
+    t, value_power, change_power = read_tags(r[96:])
+    return unfold(restored(r[64:96], change_power)), restored(r[:64], value_power), t
 
 
 def join(earlier, later):
@@ -261,10 +307,11 @@
     return moved[:, 128:] + change, moved[:, :128] + offset
 
 
-def near_kernel(r_ref, *refs):
-    traces, (send_ref, value_ref, matrix_ref) = refs[:-3], refs[-3:]
+def near_kernel(r_ref, t_ref, other_ref, send_ref, value_ref, matrix_ref):
     count = r_ref.shape[0]
-    spans = [(unfold(r_ref[j, 64:96]), r_ref[j, :64]) for j in range(count)]
+    spans = [
+        (unfold(r_ref[j, 64:] / CHANGE_SCALE), r_ref[j, :64] / VALUE_SCALE) for j in range(count)
+    ]
     before = [None] + spans[:1]
     pairs = [join(spans[j], spans[j + 1]) for j in range(0, count, 2)]
     upto = pairs[:1]
@@ -280,72 +327,68 @@
         matrix, value = before[j] if j else (jnp.zeros((64, 64), F32), jnp.zeros((64, 128), F32))
         value_ref[j] = value
         matrix_ref[j] = matrix
-    change, value = fold(total[0]), total[1]
-    trace = sum(t[...] for t in traces)
-    for i in range(send_ref.shape[0]):
-        send_ref[i, :64] = value
-        send_ref[i, 64:96] = change
-        send_ref[i, 96:] = trace
-
-
-def far_kernel(place_ref, r_ref, send_ref, value_ref, matrix_ref, t_ref):
+    put(send_ref, *total, t_ref[...] + other_ref[...])
+
+
+def far_kernel(place_ref, r_ref, send_ref, value_ref, matrix_ref):
     count = r_ref.shape[0]
     me = place_ref[0]
-    rows = lax.broadcasted_iota(jnp.int32, (8, 128), 0)
-    matrix, value = eye(64), jnp.zeros((64, 128), F32)
-    own_matrix, own_value = matrix, value
-    before = total = own = jnp.zeros((8, 128), F32)
+    span = own = (jnp.zeros((64, 64), F32), jnp.zeros((64, 128), F32))
+    before = total = mine = jnp.zeros((8, 1), F32)
     for i in range(count):
-        own_matrix = jnp.where(me == i, matrix, own_matrix)
-        own_value = jnp.where(me == i, value, own_value)
-        t = r_ref[i, 96:]
+        own = tuple(jnp.where(me == i, new, old) for new, old in zip(span, own))
+        change, value, t = take(r_ref[i])
         before = jnp.where(me == i, total, before)
-        own = jnp.where(me == i, t, own)
+        mine = jnp.where(me == i, t, mine)
         total = total + t
-        matrix, value = advance(matrix, value, unfold(r_ref[i, 64:96]), r_ref[i, :64])
-    value_ref[...] = own_value
-    matrix_ref[...] = own_matrix
+        span = join(span, (change, value)) if i else (change, value)
+    matrix_ref[...], value_ref[...] = own
     spread = jnp.sum(before, axis=0, keepdims=True)
-    t_ref[...] = jnp.where(rows == 2, spread, own)
-    change = fold(matrix - eye(64))
-    for i in range(send_ref.shape[0]):
-        send_ref[i, :64] = value
-        send_ref[i, 64:96] = change
-        send_ref[i, 96:] = total
-
-
-def back_kernel(place_ref, r_ref, far_value, far_matrix, t_ref, near_value, near_matrix, send_ref):
-    me = place_ref[0]
-    rows = lax.broadcasted_iota(jnp.int32, (8, 128), 0)
+    t = jnp.concatenate([total[:2], mine[:2], spread, jnp.zeros((3, 1), F32)], axis=0)
+    put(send_ref, *span, jnp.broadcast_to(t, (8, 128)))
+
+
+def back_kernel(
+    place_ref, strip_ref, r_ref, far_value, far_matrix, near_value, near_matrix, send_ref
+):
+    me, strip = place_ref[0], strip_ref[0]
     state = own = jnp.zeros((64, 128), F32)
-    before = total = jnp.zeros((8, 128), F32)
-    count = r_ref.shape[0]
+    before = total = mine = jnp.zeros((8, 1), F32)
+    copies = 2
+    count = r_ref.shape[0] // copies
     for i in range(count):
         own = jnp.where(me == i, state, own)
         before = jnp.where(me == i, total, before)
-        total = total + r_ref[i, 96:]
+        t = sum(read_tags(r_ref[copies * i + n, 96:])[0] for n in range(copies))
+        mine = jnp.where(me == i, t, mine)
+        total = total + t
         if i < count - 1:
-            state = state + mix(unfold(r_ref[i, 64:96]), state) + r_ref[i, :64]
-    entry = mix(far_matrix[...], own) + far_value[...]
+            change, value, _ = take(r_ref[copies * i + strip])
+            state = state + mix(change, state) + value
+    entry = own + mix(far_matrix[...], own) + far_value[...]
     near = near_matrix.shape[0]
     states = mix(near_matrix[...].reshape(near * 64, 64), entry)
-    spread = jnp.sum(before, axis=0, keepdims=True)
-    t = t_ref[...] + jnp.where(rows == 2, spread, 0.0)
+    spread = jnp.sum(before[:2], axis=0, keepdims=True)
+    t = jnp.concatenate([mine[2:5], spread, jnp.zeros((4, 1), F32)], axis=0)
+    t = jnp.broadcast_to(t, (8, 128))
     for j in range(near):
-        send_ref[j, :64] = entry + states[j * 64 : (j + 1) * 64] + near_value[j]
-        send_ref[j, 64:] = t
+        state = entry + states[j * 64 : (j + 1) * 64] + near_value[j]
+        power = block_exponent(state)
+        send_ref[j, :64] = scaled(state, power)
+        send_ref[j, 64:] = tags(t, power, power)
 
 
 def final_kernel(place_ref, me_ref, r_ref, g_ref, state_ref, log_ref):
     leading, me = place_ref[0] == 0, me_ref[0]
     count = r_ref.shape[0]
-    earlier = jnp.zeros((1, 128), F32)
-    own = jnp.zeros((8, 128), F32)
+    earlier = jnp.zeros((1, 1), F32)
+    own = jnp.zeros((8, 1), F32)
     for j in range(count):
         at = slice(j * 128, (j + 1) * 128)
-        state_ref[0, 0, :, at] = jnp.where(leading, g_ref[0, 0, :, at], r_ref[j, :64])
-        t = r_ref[j, 64:]
-        earlier = earlier + t[2:3] + jnp.where(j < me, t[0:1] + t[1:2], 0.0)
+        t, power, _ = read_tags(r_ref[j, 64:])
+        state = restored(r_ref[j, :64], power)
+        state_ref[0, 0, :, at] = jnp.where(leading, g_ref[0, 0, :, at], state)
+        earlier = earlier + t[2:3] + t[3:4] + jnp.where(j < me, t[0:1] + t[1:2], 0.0)
         own = jnp.where(me == j, t, own)
     first = earlier + own[0:1]
     second = first + own[1:2]
@@ -353,19 +396,23 @@
     log_ref[1] = -(STEP / WIDTH) * second[0, 0]
 
 
+def exchange(v, axes):
+    return lax.all_to_all(v.astype(F16), axes, 0, 0, tiled=True).astype(F32)
+
+
 def body(guess, kernels, biases, probes):
-    strips = lax.axis_size("space")
-    strip = lax.axis_index("space")
-    near = lax.axis_size("zl") * lax.axis_size("c")
+    strips = lax.axis_size(SPACE)
+    strip = lax.axis_index(SPACE)
+    near = lax.axis_size(NEAR)
     far, last = lax.axis_size("zh"), lax.axis_size("x")
     cells = guess.shape[3]
     place = lax.axis_index(TM).reshape(1)
 
-    up, down = edges(guess, probes)
+    up, down, guess, probes = edges(guess, probes)
     forward = [(i, i + 1) for i in range(strips - 1)]
     backward = [(i + 1, i) for i in range(strips - 1)]
-    low = lax.ppermute(down, "space", forward)
-    high = lax.ppermute(up, "space", backward)
+    low = lax.ppermute(down, SPACE, forward)
+    high = lax.ppermute(up, SPACE, backward)
     state, offset, change, inner = call(
         inner_kernel,
         [(64, cells), (64, cells), (32, 128), (8, 128)],
@@ -386,38 +433,43 @@
         "outer",
         20,
     )
-    got = lax.all_to_all(send, NEAR, 0, 0, tiled=True)
-    traces = [
-        lax.ppermute(trace, "space", [(i, (i + hop) % strips) for i in range(strips)])
-        for hop in range(1, strips)
-    ]
+    got = exchange(send, NEAR)
+    other = lax.ppermute(trace, "sl", [(0, 1), (1, 0)])
     send, near_value, near_matrix = call(
         near_kernel,
-        [(far, 104, 128), (near, 64, 128), (near, 64, 64)],
+        [(far, 112, 128), (near, 64, 128), (near, 64, 64)],
         0,
-        (got, trace, *traces),
+        (got, trace, other),
         "near",
         8,
     )
-    got = lax.all_to_all(send, "zh", 0, 0, tiled=True)
-    send, far_value, far_matrix, trace = call(
+    got = exchange(send, "zh")
+    send, far_value, far_matrix = call(
         far_kernel,
-        [(last, 104, 128), (64, 128), (64, 64), (8, 128)],
+        [(2 * last, 112, 128), (64, 128), (64, 64)],
         1,
         (lax.axis_index("zh").reshape(1), got),
         "far",
         8,
     )
-    got = lax.all_to_all(send, "x", 0, 0, tiled=True)
+    got = exchange(send, ("x", "sh"))
     (send,) = call(
         back_kernel,
-        [(near, 72, 128)],
-        1,
-        (lax.axis_index("x").reshape(1), got, far_value, far_matrix, trace, near_value, near_matrix),
+        [(near, 80, 128)],
+        2,
+        (
+            lax.axis_index("x").reshape(1),
+            lax.axis_index("sh").reshape(1),
+            got,
+            far_value,
+            far_matrix,
+            near_value,
+            near_matrix,
+        ),
         "back",
         8,
     )
-    got = lax.all_to_all(send, NEAR, 0, 0, tiled=True)
+    got = exchange(send, NEAR)
     return call(
         final_kernel,
         [(1, 1, 64, cells), (2,)],
@@ -430,18 +482,18 @@
 
 def solution(mesh):
     finer = Mesh(
-        mesh.devices.reshape(4, 4, 4, 2, mesh.shape["space"]), ("x", "zh", "zl", "c", "space")
+        mesh.devices.reshape(4, 4, 4, 2, 2, 2), ("x", "zh", "zl", "c", "sh", "sl")
     )
     placed = (
-        P(TM, None, None, "space"),
+        P(TM, None, None, SPACE),
         P(TM, None, None),
         P(TM, None),
-        P(None, None, None, "space"),
+        P(None, None, None, SPACE),
     )
     return jax.shard_map(
         body,
         mesh=finer,
         in_specs=placed,
-        out_specs=(P(TM, None, None, "space"), P(TM)),
+        out_specs=(P(TM, None, None, SPACE), P(TM)),
         check_vma=False,
     )

time: 95.5 us -> 84.7 us (0.89)
  starting transfers between devices: 22.7 us -> 16.5 us
  blocking collectives: 56.3 us -> 51.5 us
  local copies, waits for them, and re-layouts: 2.57 us -> 0.67 us
  waiting for transfers between devices: 3.57 us -> 5.42 us
    ppermute x5 -> x3, starting transfers between devices: 14.3 us -> 7.96 us  [the longest x1 4.02 us: body(): low = lax.ppermute(down, SPACE, forward)]
    all_to_all x3, blocking collectives: 56.3 us -> 51.5 us  [exchange(): return lax.all_to_all(v.astype(F16), axes, 0, 0, tiled=True).astype(F32)]
    all_to_all x1, waiting for transfers between devices: 0.01 us -> 3.89 us  [exchange(): return lax.all_to_all(v.astype(F16), axes, 0, 0, tiled=True).astype(F32)]
    ppermute x5 -> x3, waiting for transfers between devices: 3.56 us -> 1.54 us  [the longest x1 1.53 us: body(): high = lax.ppermute(up, SPACE, backward)]
    unnamed x10 -> x4, local copies, waits for them, and re-layouts: 2.57 us -> 0.67 us
  transfers between devices with their start and end apart: 6 -> 4, of which waited for: 2 -> 2; matrix products, arithmetic and copies ran while one was open for 0% -> 0% of each run, Pallas kernels for 2% -> 2%
where the time goes in v3:
time: 84.7 us; the launch traced here: 84.3 us
  blocking collectives  51.5 us (61%)
  starting transfers between devices  16.5 us (19%)
  Pallas kernels  8.58 us (10%)
  waiting for transfers between devices  5.42 us (6%)
  other arithmetic  0.88 us (1%)
    all_to_all x3, blocking collectives, exchange(): return lax.all_to_all(v.astype(F16), axes, 0, 0, tiled=True).astype(F32)  51.5 us
    all_to_all x1, starting transfers between devices, exchange(): return lax.all_to_all(v.astype(F16), axes, 0, 0, tiled=True).astype(F32)  8.55 us
    pallas_call x6, Pallas kernels, call(): pl.pallas_call(kernel, in_specs=[scalars()] * places + [whole()] * (len(a...  7.49 us
    ppermute x1, starting transfers between devices, body(): low = lax.ppermute(down, SPACE, forward)  4.02 us
    all_to_all x1, waiting for transfers between devices, exchange(): return lax.all_to_all(v.astype(F16), axes, 0, 0, tiled=True).astype(F32)  3.89 us
    ppermute x1, starting transfers between devices, body(): other = lax.ppermute(trace, 'sl', [(0, 1), (1, 0)])  2.64 us
  transfers between devices with their start and end apart: 4, of which 2 were waited for; matrix products, arithmetic and copies ran while one was open for 0% of the time, Pallas kernels for 2%

profile of v3, /device:TPU:1, one launch (start us, length us, event | category | flops | bytes accessed | tf_op | source)
XLA Modules:
  0.0 84.3 jit_solution(15446765215445577864)
XLA Ops:
  0.6 0.0 copy-start
  0.6 1.1 %edges.1 = (f32[128,128]{1,0:T(8,128)S(1)}, f32[128,128]{1,0:T(8,128)S(1)}, f32[1,1,64,1024]{3,2,1,0:T(8,128)S(1)}, bf16[2,1,64,1024]{3,2,1,0:T(8,128)(2,1)S(1)}) custom-call(f32[1,1,64,1024]{3,2,1,0:T(8,128)} %g_ref.1, bf16[2,1,64,1024]{3,2,1,0:T(8,128)(2,1)} %p_ref.1), custom_call_target="tpu_custom_call" | custom-call | tf_op jit(solution)/shard_map/edges/pallas_call | solution.py:78
  1.7 4.0 %collective-permute-start = (f32[128,128]{1,0:T(8,128)S(1)}, f32[128,128]{1,0:T(8,128)S(1)}, u32[]{:S(2)}, u32[]{:S(2)}) collective-permute-start(f32[128,128]{1,0:T(8,128)S(1)} %get-tuple-element.19), channel_id=1, source_target_pairs={{0,1},{1,2},{2,3},{4,5},{5,6},{6,7},{8,9},{9,10},{10,11},{12,13},{... | collective-permute-start | bytes 196616 | tf_op jit(solution)/shard_map/ppermute | solution.py:414
  5.8 1.3 %collective-permute-start.1 = (f32[128,128]{1,0:T(8,128)S(1)}, f32[128,128]{1,0:T(8,128)S(1)}, u32[]{:S(2)}, u32[]{:S(2)}) collective-permute-start(f32[128,128]{1,0:T(8,128)S(1)} %get-tuple-element.20), channel_id=1, source_target_pairs={{1,0},{2,1},{3,2},{5,4},{6,5},{7,6},{9,8},{10,9},{11,10},{13,12},{... | collective-permute-start | bytes 196616 | tf_op jit(solution)/shard_map/ppermute | solution.py:415
  7.1 0.0 copy-start.1
  7.1 0.0 copy-done
  7.1 0.7 copy-done.1
  7.8 1.5 %inner.1 = (f32[64,1024]{1,0:T(8,128)S(1)}, f32[64,1024]{1,0:T(8,128)S(1)}, f32[32,128]{1,0:T(8,128)S(1)}, f32[8,128]{1,0:T(8,128)S(1)}) custom-call(s32[1]{0:T(128)} %bitcast.place_ref, f32[1,1,64,1024]{3,2,1,0:T(8,128)S(1)} %get-tuple-element.18.g_ref, bf16[2,1,64,1024]{3,2,1,0:T(8,128)(2,1)S(1)} %get-tuple-element.21.p_ref, ...), custom_call_target="tpu_custom_call" | custom-call | flops 450000000 | bytes 2000000 | tf_op jit(solution)/shard_map/inner/pallas_call | solution.py:244
  9.2 0.0 collective-permute-done.low_ref
  9.2 1.5 %collective-permute-done.1.high_ref = f32[128,128]{1,0:T(8,128)S(1)} collective-permute-done((f32[128,128]{1,0:T(8,128)S(1)}, f32[128,128]{1,0:T(8,128)S(1)}, u32[]{:S(2)}, u32[]{:S(2)}) %collective-permute-start.1) | collective-permute-done | bytes 65568 | tf_op jit(solution)/shard_map/ppermute | solution.py:415
  10.8 2.2 %outer.1 = (f32[8,96,128]{2,1,0:T(8,128)S(1)}, f32[8,128]{1,0:T(8,128)S(1)}) custom-call(s32[1]{0:T(128)} %bitcast.5.strip_ref, f32[1,1,64,1024]{3,2,1,0:T(8,128)S(1)} %get-tuple-element.18.g_ref, f32[128,128]{1,0:T(8,128)S(1)} %collective-permute-done.low_ref, f32[128,128]{1,0:T(8,128)S(1)} %collective-permute-done.1.high_ref, ...), custom_call_target="tpu_custom_call" | custom-call | tf_op jit(solution)/shard_map/outer/pallas_call | solution.py:244
  12.9 0.7 convert_element_type.24
  13.7 8.6 %all-to-all-start = ((f16[8,96,128]{2,1,0:T(8,128)(2,1)}), f16[8,96,128]{2,1,0:T(8,128)(2,1)S(1)}, u32[]{:S(2)}, u32[]{:S(2)}) async-start(f16[8,96,128]{2,1,0:T(8,128)(2,1)} %convert_element_type.24), calls=%async_computation | async-start | bytes 393216 | tf_op jit(solution)/shard_map/all_to_all | solution.py:400
  22.2 2.6 %collective-permute-start.2 = (f32[8,128]{1,0:T(8,128)S(1)}, f32[8,128]{1,0:T(8,128)S(1)}, u32[]{:S(2)}, u32[]{:S(2)}) collective-permute-start(f32[8,128]{1,0:T(8,128)S(1)} %get-tuple-element.27.t_ref), channel_id=1, source_target_pairs={{0,1},{1,0},{2,3},{3,2},{4,5},{5,4},{6,7},{7,6},{8,9},{9,8},{10,11... | collective-permute-start | bytes 12296 | tf_op jit(solution)/shard_map/ppermute | solution.py:437
  24.9 3.9 %all-to-all-done = f16[8,96,128]{2,1,0:T(8,128)(2,1)S(1)} async-done(((f16[8,96,128]{2,1,0:T(8,128)(2,1)}), f16[8,96,128]{2,1,0:T(8,128)(2,1)S(1)}, u32[]{:S(2)}, u32[]{:S(2)}) %all-to-all-start) | async-done | bytes 196640 | tf_op jit(solution)/shard_map/all_to_all | solution.py:400
  28.8 0.0 collective-permute-done.2.other_ref
  28.8 0.9 %near.1 = (f32[4,112,128]{2,1,0:T(8,128)S(1)}, f32[8,64,128]{2,1,0:T(8,128)S(1)}, f32[8,64,64]{2,1,0:T(8,128)S(1)}) custom-call(f32[8,96,128]{2,1,0:T(8,128)S(1)} %convert_element_type.25.r_ref, f32[8,128]{1,0:T(8,128)S(1)} %get-tuple-element.27.t_ref, f32[8,128]{1,0:T(8,128)S(1)} %collective-permute-done.2.other_ref), custom_call_target="tpu_custom_call" | custom-call | tf_op jit(solution)/shard_map/near/pallas_call | solution.py:244
  29.7 23.6 %all_to_all.20 = f16[4,112,128]{2,1,0:T(8,128)(2,1)S(1)} all-to-all(f16[4,112,128]{2,1,0:T(8,128)(2,1)S(1)} %convert_element_type.26), channel_id=1, replica_groups=mesh['x'=4,'zh'=4,'zl'=4,'c'=2,'sh'=2,'sl'=2] {'zh'}, dimensions={0} | all-to-all | bytes 229376 | tf_op jit(solution)/shard_map/all_to_all | solution.py:400
  53.3 0.9 %far.1 = (f32[8,112,128]{2,1,0:T(8,128)S(1)}, f32[64,128]{1,0:T(8,128)S(1)}, f32[64,64]{1,0:T(8,128)S(1)}) custom-call(s32[1]{0:T(128)} %bitcast.4.place_ref, f32[4,112,128]{2,1,0:T(8,128)S(1)} %convert_element_type.27.r_ref), custom_call_target="tpu_custom_call" | custom-call | tf_op jit(solution)/shard_map/far/pallas_call | solution.py:244
  54.2 13.3 %all_to_all.21 = f16[8,112,128]{2,1,0:T(8,128)(2,1)S(1)} all-to-all(f16[8,112,128]{2,1,0:T(8,128)(2,1)S(1)} %convert_element_type.28), channel_id=1, replica_groups=mesh['x'=4,'zh'=4,'zl'=4,'c'=2,'sh'=2,'sl'=2] {'x','sh'}, dimensions={0} | all-to-all | bytes 458752 | tf_op jit(solution)/shard_map/all_to_all | solution.py:400
  67.6 1.3 %back.1 = f32[8,80,128]{2,1,0:T(8,128)S(1)} custom-call(s32[1]{0:T(128)} %bitcast.2.place_ref, s32[1]{0:T(128)} %bitcast.3.strip_ref, f32[8,112,128]{2,1,0:T(8,128)S(1)} %convert_element_type.29.r_ref, f32[64,128]{1,0:T(8,128)S(1)} %get-tuple-element.30.far_value, f32[64,64]{1,0:T(8,128)S(1)} %get-tuple-element.31.far_matrix, ...), custom_call_target="tpu_custom_call" | custom-call | tf_op jit(solution)/shard_map/back/pallas_call | solution.py:244
  68.9 14.6 %all_to_all.22 = f16[8,80,128]{2,1,0:T(8,128)(2,1)S(1)} all-to-all(f16[8,80,128]{2,1,0:T(8,128)(2,1)S(1)} %convert_element_type.30), channel_id=1, replica_groups=mesh['x'=4,'zh'=4,'zl'=4,'c'=2,'sh'=2,'sl'=2] {'zl','c'}, dimensions={0} | all-to-all | bytes 327680 | tf_op jit(solution)/shard_map/all_to_all | solution.py:400
  83.5 0.9 %final.1 = (f32[1,1,64,1024]{3,2,1,0:T(8,128)}, f32[2]{0:T(128)}) custom-call(s32[1]{0:T(128)} %bitcast.place_ref, s32[1]{0:T(128)} %bitcast.1.me_ref, f32[8,80,128]{2,1,0:T(8,128)S(1)} %convert_element_type.31.r_ref, f32[1,1,64,1024]{3,2,1,0:T(8,128)S(1)} %get-tuple-element.18.g_ref), custom_call_target="tpu_custom_call" | custom-call | tf_op jit(solution)/shard_map/final/pallas_call | solution.py:244
  (7 shorter events, 0.2 us)
Async XLA Ops:
  0.6 6.5 %copy-start = (bf16[2,64,576]{2,1,0:T(8,128)(2,1)S(1)}, bf16[2,64,576]{2,1,0:T(8,128)(2,1)}, u32[]{:S(2)}) copy-start(bf16[2,64,576]{2,1,0:T(8,128)(2,1)} %k_ref.3) | copy-start | bytes 442372
  1.7 7.5 %collective-permute-start = (f32[128,128]{1,0:T(8,128)S(1)}, f32[128,128]{1,0:T(8,128)S(1)}, u32[]{:S(2)}, u32[]{:S(2)}) collective-permute-start(f32[128,128]{1,0:T(8,128)S(1)} %get-tuple-element.19), channel_id=1, source_target_pairs={{0,1},{1,2},{2,3},{4,5},{5,6},{6,7},{8,9},{9,10},{10,11},{12,13},{... | collective-permute-start | bytes 196616 | tf_op jit(solution)/shard_map/ppermute | solution.py:414
  5.8 5.0 %collective-permute-start.1 = (f32[128,128]{1,0:T(8,128)S(1)}, f32[128,128]{1,0:T(8,128)S(1)}, u32[]{:S(2)}, u32[]{:S(2)}) collective-permute-start(f32[128,128]{1,0:T(8,128)S(1)} %get-tuple-element.20), channel_id=1, source_target_pairs={{1,0},{2,1},{3,2},{5,4},{6,5},{7,6},{9,8},{10,9},{11,10},{13,12},{... | collective-permute-start | bytes 196616 | tf_op jit(solution)/shard_map/ppermute | solution.py:415
  7.1 0.7 copy-start.1
  13.7 15.1 %all-to-all-start = ((f16[8,96,128]{2,1,0:T(8,128)(2,1)}), f16[8,96,128]{2,1,0:T(8,128)(2,1)S(1)}, u32[]{:S(2)}, u32[]{:S(2)}) async-start(f16[8,96,128]{2,1,0:T(8,128)(2,1)} %convert_element_type.24), calls=%async_computation | async-start | bytes 393216 | tf_op jit(solution)/shard_map/all_to_all | solution.py:400
  22.2 6.6 %collective-permute-start.2 = (f32[8,128]{1,0:T(8,128)S(1)}, f32[8,128]{1,0:T(8,128)S(1)}, u32[]{:S(2)}, u32[]{:S(2)}) collective-permute-start(f32[8,128]{1,0:T(8,128)S(1)} %get-tuple-element.27.t_ref), channel_id=1, source_target_pairs={{0,1},{1,0},{2,3},{3,2},{4,5},{5,4},{6,7},{7,6},{8,9},{9,8},{10,11... | collective-permute-start | bytes 12296 | tf_op jit(solution)/shard_map/ppermute | solution.py:437

commit v4 on v3

--- a/solution.py
+++ b/solution.py
@@ -55,51 +55,51 @@
     ).astype(F32)
 
 
-def edge_kernel(g_ref, p_ref, up_ref, down_ref, gv_ref, pv_ref, sems):
+def edge_kernel(g_ref, p_ref, k_ref, up_ref, down_ref, kv_ref, p_first, p_last, sems):
     end = g_ref.shape[3] - 128
+    first, last = pl.ds(0, 128), pl.ds(end, 128)
     copies = [
-        pltpu.make_async_copy(p_ref, pv_ref, sems.at[0]),
-        pltpu.make_async_copy(g_ref, gv_ref, sems.at[1]),
+        pltpu.make_async_copy(p_ref.at[:, 0, :, first], p_first, sems.at[0]),
+        pltpu.make_async_copy(p_ref.at[:, 0, :, last], p_last, sems.at[1]),
+        pltpu.make_async_copy(g_ref.at[0, 0, :, first], up_ref.at[pl.ds(0, 64)], sems.at[2]),
+        pltpu.make_async_copy(g_ref.at[0, 0, :, last], down_ref.at[pl.ds(0, 64)], sems.at[3]),
+        pltpu.make_async_copy(k_ref, kv_ref, sems.at[4]),
     ]
     for copy in copies:
         copy.start()
-    copies[0].wait()
-    first = [pv_ref[n, 0, :, :WIDTH].astype(F32) for n in range(2)]
-    last = [pv_ref[n, 0, :, end + WIDTH :].astype(F32) for n in range(2)]
-    up_ref[64:] = jnp.concatenate(first, axis=1)
-    down_ref[64:] = jnp.concatenate(last, axis=1)
-    copies[1].wait()
-    up_ref[:64] = gv_ref[0, 0, :, :128]
-    down_ref[:64] = gv_ref[0, 0, :, end:]
-
-
-def edges(guess, probes):
-    held = [pltpu.with_memory_space_constraint(v, pltpu.HBM) for v in (guess, probes)]
+    for copy in copies:
+        copy.wait()
+    up_ref[64:] = jnp.concatenate([p_first[n].astype(F32)[:, :WIDTH] for n in range(2)], axis=1)
+    down_ref[64:] = jnp.concatenate([p_last[n].astype(F32)[:, WIDTH:] for n in range(2)], axis=1)
+
+
+def edges(guess, probes, kernels):
+    held = [pltpu.with_memory_space_constraint(v, pltpu.HBM) for v in (guess, probes, kernels)]
     return pl.pallas_call(
         edge_kernel,
-        in_specs=[pl.BlockSpec(memory_space=pltpu.HBM)] * 2,
-        out_specs=[whole()] * 4,
+        in_specs=[pl.BlockSpec(memory_space=pltpu.HBM)] * 3,
+        out_specs=[whole()] * 3,
         out_shape=[jax.ShapeDtypeStruct((128, 128), F32)] * 2
-        + [jax.ShapeDtypeStruct(guess.shape, F32), jax.ShapeDtypeStruct(probes.shape, BF16)],
-        scratch_shapes=[pltpu.SemaphoreType.DMA((2,))],
-        compiler_params=pltpu.CompilerParams(vmem_limit_bytes=4 << 20),
+        + [jax.ShapeDtypeStruct(kernels.shape, BF16)],
+        scratch_shapes=[pltpu.VMEM((2, 64, 128), BF16)] * 2 + [pltpu.SemaphoreType.DMA((5,))],
+        compiler_params=pltpu.CompilerParams(vmem_limit_bytes=2 << 20),
         name="edges",
     )(*held)
 
 
 def taps(v):
     n = v.shape[1]
-    column = lax.broadcasted_iota(jnp.int32, v.shape, 1) & (WIDTH - 1)
-    left = pltpu.roll(jnp.where(column == WIDTH - 1, 0.0, v), 1, 1)
-    right = pltpu.roll(jnp.where(column == 0, 0.0, v), n - 1, 1)
+    column = lax.broadcasted_iota(jnp.int32, (16, n), 1) & (WIDTH - 1)
+    keep = [jnp.where(column == edge, 0.0, 1.0).astype(BF16) for edge in (WIDTH - 1, 0)]
+    keep = [jnp.concatenate([k] * (v.shape[0] // 16), axis=0) for k in keep]
+    left = pltpu.roll(v * keep[0], 1, 1)
+    right = pltpu.roll(v * keep[1], n - 1, 1)
     rows = []
     for part in (left, v, right):
         above = pltpu.roll(part, WIDTH, 1)
         below = jnp.concatenate([above[:, 128:], above[:, :128]], axis=1)
         rows.append((above, part, below))
-    return jnp.concatenate(
-        [rows[dx][dy].astype(BF16) for dy in range(3) for dx in range(3)], axis=0
-    )
+    return jnp.concatenate([rows[dx][dy] for dy in range(3) for dx in range(3)], axis=0)
 
 
 def rounded(v):
@@ -107,7 +107,7 @@
 
 
 def convolve(kernel, v, at=None):
-    stack = taps(rounded(v))
+    stack = taps(v.astype(BF16))
     return jnp.dot(kernel, stack if at is None else stack[:, at], preferred_element_type=F32)
 
 
@@ -274,14 +274,15 @@
     unit = t * jnp.exp2(-power)
     coarse = rounded(unit)
     fine = 256.0 * (unit - coarse)
-    top = jnp.where(lane < 64, coarse, power)
-    low = jnp.where(lane < 64, fine, jnp.where(lane < 96, value_power, change_power))
-    return jnp.concatenate([top, low], axis=0)
+    scales = jnp.where(lane < 112, value_power, change_power)
+    return jnp.where(
+        lane < 32, coarse, jnp.where(lane < 64, fine, jnp.where(lane < 96, power, scales))
+    )
 
 
 def read_tags(r):
-    t = (r[:8, :1] + r[8:, :1] / 256.0) * jnp.exp2(r[:8, 64:65])
-    return t, r[8:9, 64:65], r[8:9, 96:97]
+    t = (r[:, :1] + r[:, 32:33] / 256.0) * jnp.exp2(r[:, 64:65])
+    return t, r[:1, 96:97], r[:1, 112:113]
 
 
 def put(ref, change, value, t):
@@ -371,11 +372,12 @@
     spread = jnp.sum(before[:2], axis=0, keepdims=True)
     t = jnp.concatenate([mine[2:5], spread, jnp.zeros((4, 1), F32)], axis=0)
     t = jnp.broadcast_to(t, (8, 128))
+    states = [entry + states[j * 64 : (j + 1) * 64] + near_value[j] for j in range(near)]
+    power = block_exponent(functools.reduce(jnp.maximum, [jnp.abs(state) for state in states]))
+    extra = tags(t, power, power)
     for j in range(near):
-        state = entry + states[j * 64 : (j + 1) * 64] + near_value[j]
-        power = block_exponent(state)
-        send_ref[j, :64] = scaled(state, power)
-        send_ref[j, 64:] = tags(t, power, power)
+        send_ref[j, :64] = scaled(states[j], power)
+        send_ref[j, 64:] = extra
 
 
 def final_kernel(place_ref, me_ref, r_ref, g_ref, state_ref, log_ref):
@@ -408,7 +410,7 @@
     cells = guess.shape[3]
     place = lax.axis_index(TM).reshape(1)
 
-    up, down, guess, probes = edges(guess, probes)
+    up, down, kernels = edges(guess, probes, kernels)
     forward = [(i, i + 1) for i in range(strips - 1)]
     backward = [(i + 1, i) for i in range(strips - 1)]
     low = lax.ppermute(down, SPACE, forward)
@@ -437,7 +439,7 @@
     other = lax.ppermute(trace, "sl", [(0, 1), (1, 0)])
     send, near_value, near_matrix = call(
         near_kernel,
-        [(far, 112, 128), (near, 64, 128), (near, 64, 64)],
+        [(far, 104, 128), (near, 64, 128), (near, 64, 64)],
         0,
         (got, trace, other),
         "near",
@@ -446,7 +448,7 @@
     got = exchange(send, "zh")
     send, far_value, far_matrix = call(
         far_kernel,
-        [(2 * last, 112, 128), (64, 128), (64, 64)],
+        [(2 * last, 104, 128), (64, 128), (64, 64)],
         1,
         (lax.axis_index("zh").reshape(1), got),
         "far",
@@ -455,7 +457,7 @@
     got = exchange(send, ("x", "sh"))
     (send,) = call(
         back_kernel,
-        [(near, 80, 128)],
+        [(near, 72, 128)],
         2,
         (
             lax.axis_index("x").reshape(1),

time: 84.7 us -> 84.2 us (level)
  no operation moved by 1% of the time
where the time goes in v4:
time: 84.2 us; the launch traced here: 83.8 us
  blocking collectives  51.1 us (61%)
  starting transfers between devices  16.5 us (20%)
  Pallas kernels  8.43 us (10%)
  waiting for transfers between devices  5.44 us (6%)
  other arithmetic  0.87 us (1%)
    all_to_all x3, blocking collectives, exchange(): return lax.all_to_all(v.astype(F16), axes, 0, 0, tiled=True).astype(F32)  51.1 us
    all_to_all x1, starting transfers between devices, exchange(): return lax.all_to_all(v.astype(F16), axes, 0, 0, tiled=True).astype(F32)  8.55 us
    pallas_call x6, Pallas kernels, call(): pl.pallas_call(kernel, in_specs=[scalars()] * places + [whole()] * (len(a...  7.26 us
    ppermute x1, starting transfers between devices, body(): low = lax.ppermute(down, SPACE, forward)  4.02 us
    all_to_all x1, waiting for transfers between devices, exchange(): return lax.all_to_all(v.astype(F16), axes, 0, 0, tiled=True).astype(F32)  3.88 us
    ppermute x1, starting transfers between devices, body(): other = lax.ppermute(trace, 'sl', [(0, 1), (1, 0)])  2.64 us
  transfers between devices with their start and end apart: 4, of which 2 were waited for; matrix products, arithmetic and copies ran while one was open for 0% of the time, Pallas kernels for 2%

profile of v4, /device:TPU:1, one launch (start us, length us, event | category | flops | bytes accessed | tf_op | source)
XLA Modules:
  0.0 83.8 jit_solution(12917017004571979761)
XLA Ops:
  0.6 0.0 copy-start
  0.6 0.0 copy-start.1
  0.6 1.2 %edges.1 = (f32[128,128]{1,0:T(8,128)S(1)}, f32[128,128]{1,0:T(8,128)S(1)}, bf16[2,64,576]{2,1,0:T(8,128)(2,1)S(1)}) custom-call(f32[1,1,64,1024]{3,2,1,0:T(8,128)} %g_ref.7, bf16[2,1,64,1024]{3,2,1,0:T(8,128)(2,1)} %p_ref.5, bf16[2,64,576]{2,1,0:T(8,128)(2,1)} %k_ref.1), custom_call_target="tpu_custom_call" | custom-call | tf_op jit(solution)/shard_map/edges/pallas_call | solution.py:78
  1.8 4.0 %collective-permute-start = (f32[128,128]{1,0:T(8,128)S(1)}, f32[128,128]{1,0:T(8,128)S(1)}, u32[]{:S(2)}, u32[]{:S(2)}) collective-permute-start(f32[128,128]{1,0:T(8,128)S(1)} %get-tuple-element.17), channel_id=1, source_target_pairs={{0,1},{1,2},{2,3},{4,5},{5,6},{6,7},{8,9},{9,10},{10,11},{12,13},{... | collective-permute-start | bytes 196616 | tf_op jit(solution)/shard_map/ppermute | solution.py:416
  5.9 1.3 %collective-permute-start.1 = (f32[128,128]{1,0:T(8,128)S(1)}, f32[128,128]{1,0:T(8,128)S(1)}, u32[]{:S(2)}, u32[]{:S(2)}) collective-permute-start(f32[128,128]{1,0:T(8,128)S(1)} %get-tuple-element.18), channel_id=1, source_target_pairs={{1,0},{2,1},{3,2},{5,4},{6,5},{7,6},{9,8},{10,9},{11,10},{13,12},{... | collective-permute-start | bytes 196616 | tf_op jit(solution)/shard_map/ppermute | solution.py:417
  7.2 0.0 copy-start.2
  7.2 0.0 copy-done
  7.2 0.0 copy-done.1
  7.2 0.7 copy-done.2
  7.9 1.4 %inner.1 = (f32[64,1024]{1,0:T(8,128)S(1)}, f32[64,1024]{1,0:T(8,128)S(1)}, f32[32,128]{1,0:T(8,128)S(1)}, f32[8,128]{1,0:T(8,128)S(1)}) custom-call(s32[1]{0:T(128)} %bitcast.place_ref, f32[1,1,64,1024]{3,2,1,0:T(8,128)S(1)} %copy-done, bf16[2,1,64,1024]{3,2,1,0:T(8,128)(2,1)S(1)} %copy-done.1, bf16[2,64,576]{2,1,0:T(8,128)(2,1)S(1)} %get-tuple-element.19.k_ref, ...), custom_call_target="tpu_custom_call" | custom-call | flops 450000000 | bytes 2000000 | tf_op jit(solution)/shard_map/inner/pallas_call | solution.py:244
  9.3 0.0 collective-permute-done.low_ref
  9.3 1.6 %collective-permute-done.1.high_ref = f32[128,128]{1,0:T(8,128)S(1)} collective-permute-done((f32[128,128]{1,0:T(8,128)S(1)}, f32[128,128]{1,0:T(8,128)S(1)}, u32[]{:S(2)}, u32[]{:S(2)}) %collective-permute-start.1) | collective-permute-done | bytes 65568 | tf_op jit(solution)/shard_map/ppermute | solution.py:417
  10.9 1.9 %outer.1 = (f32[8,96,128]{2,1,0:T(8,128)S(1)}, f32[8,128]{1,0:T(8,128)S(1)}) custom-call(s32[1]{0:T(128)} %bitcast.5.strip_ref, f32[1,1,64,1024]{3,2,1,0:T(8,128)S(1)} %copy-done, f32[128,128]{1,0:T(8,128)S(1)} %collective-permute-done.low_ref, f32[128,128]{1,0:T(8,128)S(1)} %collective-permute-done.1.high_ref, bf16[2,1,64,1024]{3,2,1,0:T(8,128)(2,1)S(1)} %copy-done.1, ...), custom_call_target="tpu_custom_call" | custom-call | tf_op jit(solution)/shard_map/outer/pallas_call | solution.py:244
  12.8 0.7 convert_element_type.24
  13.5 8.6 %all-to-all-start = ((f16[8,96,128]{2,1,0:T(8,128)(2,1)}), f16[8,96,128]{2,1,0:T(8,128)(2,1)S(1)}, u32[]{:S(2)}, u32[]{:S(2)}) async-start(f16[8,96,128]{2,1,0:T(8,128)(2,1)} %convert_element_type.24), calls=%async_computation | async-start | bytes 393216 | tf_op jit(solution)/shard_map/all_to_all | solution.py:402
  22.1 2.6 %collective-permute-start.2 = (f32[8,128]{1,0:T(8,128)S(1)}, f32[8,128]{1,0:T(8,128)S(1)}, u32[]{:S(2)}, u32[]{:S(2)}) collective-permute-start(f32[8,128]{1,0:T(8,128)S(1)} %get-tuple-element.25.t_ref), channel_id=1, source_target_pairs={{0,1},{1,0},{2,3},{3,2},{4,5},{5,4},{6,7},{7,6},{8,9},{9,8},{10,11... | collective-permute-start | bytes 12296 | tf_op jit(solution)/shard_map/ppermute | solution.py:439
  24.7 3.9 %all-to-all-done = f16[8,96,128]{2,1,0:T(8,128)(2,1)S(1)} async-done(((f16[8,96,128]{2,1,0:T(8,128)(2,1)}), f16[8,96,128]{2,1,0:T(8,128)(2,1)S(1)}, u32[]{:S(2)}, u32[]{:S(2)}) %all-to-all-start) | async-done | bytes 196640 | tf_op jit(solution)/shard_map/all_to_all | solution.py:402
  28.6 0.0 collective-permute-done.2.other_ref
  28.7 0.9 %near.1 = (f32[4,104,128]{2,1,0:T(8,128)S(1)}, f32[8,64,128]{2,1,0:T(8,128)S(1)}, f32[8,64,64]{2,1,0:T(8,128)S(1)}) custom-call(f32[8,96,128]{2,1,0:T(8,128)S(1)} %convert_element_type.25.r_ref, f32[8,128]{1,0:T(8,128)S(1)} %get-tuple-element.25.t_ref, f32[8,128]{1,0:T(8,128)S(1)} %collective-permute-done.2.other_ref), custom_call_target="tpu_custom_call" | custom-call | tf_op jit(solution)/shard_map/near/pallas_call | solution.py:244
  29.6 24.5 %all_to_all.20 = f16[4,104,128]{2,1,0:T(8,128)(2,1)S(1)} all-to-all(f16[4,104,128]{2,1,0:T(8,128)(2,1)S(1)} %convert_element_type.26), channel_id=1, replica_groups=mesh['x'=4,'zh'=4,'zl'=4,'c'=2,'sh'=2,'sl'=2] {'zh'}, dimensions={0} | all-to-all | bytes 212992 | tf_op jit(solution)/shard_map/all_to_all | solution.py:402
  54.1 0.9 %far.1 = (f32[8,104,128]{2,1,0:T(8,128)S(1)}, f32[64,128]{1,0:T(8,128)S(1)}, f32[64,64]{1,0:T(8,128)S(1)}) custom-call(s32[1]{0:T(128)} %bitcast.4.place_ref, f32[4,104,128]{2,1,0:T(8,128)S(1)} %convert_element_type.27.r_ref), custom_call_target="tpu_custom_call" | custom-call | tf_op jit(solution)/shard_map/far/pallas_call | solution.py:244
  55.0 13.2 %all_to_all.21 = f16[8,104,128]{2,1,0:T(8,128)(2,1)S(1)} all-to-all(f16[8,104,128]{2,1,0:T(8,128)(2,1)S(1)} %convert_element_type.28), channel_id=1, replica_groups=mesh['x'=4,'zh'=4,'zl'=4,'c'=2,'sh'=2,'sl'=2] {'x','sh'}, dimensions={0} | all-to-all | bytes 425984 | tf_op jit(solution)/shard_map/all_to_all | solution.py:402
  68.3 1.3 %back.1 = f32[8,72,128]{2,1,0:T(8,128)S(1)} custom-call(s32[1]{0:T(128)} %bitcast.2.place_ref, s32[1]{0:T(128)} %bitcast.3.strip_ref, f32[8,104,128]{2,1,0:T(8,128)S(1)} %convert_element_type.29.r_ref, f32[64,128]{1,0:T(8,128)S(1)} %get-tuple-element.28.far_value, f32[64,64]{1,0:T(8,128)S(1)} %get-tuple-element.29.far_matrix, ...), custom_call_target="tpu_custom_call" | custom-call | tf_op jit(solution)/shard_map/back/pallas_call | solution.py:244
  69.6 13.4 %all_to_all.22 = f16[8,72,128]{2,1,0:T(8,128)(2,1)S(1)} all-to-all(f16[8,72,128]{2,1,0:T(8,128)(2,1)S(1)} %convert_element_type.30), channel_id=1, replica_groups=mesh['x'=4,'zh'=4,'zl'=4,'c'=2,'sh'=2,'sl'=2] {'zl','c'}, dimensions={0} | all-to-all | bytes 294912 | tf_op jit(solution)/shard_map/all_to_all | solution.py:402
  83.0 0.9 %final.1 = (f32[1,1,64,1024]{3,2,1,0:T(8,128)}, f32[2]{0:T(128)}) custom-call(s32[1]{0:T(128)} %bitcast.place_ref, s32[1]{0:T(128)} %bitcast.1.me_ref, f32[8,72,128]{2,1,0:T(8,128)S(1)} %convert_element_type.31.r_ref, f32[1,1,64,1024]{3,2,1,0:T(8,128)S(1)} %copy-done), custom_call_target="tpu_custom_call" | custom-call | tf_op jit(solution)/shard_map/final/pallas_call | solution.py:244
  (7 shorter events, 0.2 us)
Async XLA Ops:
  0.6 6.6 %copy-start = (f32[1,1,64,1024]{3,2,1,0:T(8,128)S(1)}, f32[1,1,64,1024]{3,2,1,0:T(8,128)}, u32[]{:S(2)}) copy-start(f32[1,1,64,1024]{3,2,1,0:T(8,128)} %g_ref.7) | copy-start | bytes 786436
  0.6 6.6 %copy-start.1 = (bf16[2,1,64,1024]{3,2,1,0:T(8,128)(2,1)S(1)}, bf16[2,1,64,1024]{3,2,1,0:T(8,128)(2,1)}, u32[]{:S(2)}) copy-start(bf16[2,1,64,1024]{3,2,1,0:T(8,128)(2,1)} %p_ref.5) | copy-start | bytes 786436
  1.8 7.5 %collective-permute-start = (f32[128,128]{1,0:T(8,128)S(1)}, f32[128,128]{1,0:T(8,128)S(1)}, u32[]{:S(2)}, u32[]{:S(2)}) collective-permute-start(f32[128,128]{1,0:T(8,128)S(1)} %get-tuple-element.17), channel_id=1, source_target_pairs={{0,1},{1,2},{2,3},{4,5},{5,6},{6,7},{8,9},{9,10},{10,11},{12,13},{... | collective-permute-start | bytes 196616 | tf_op jit(solution)/shard_map/ppermute | solution.py:416
  5.9 5.0 %collective-permute-start.1 = (f32[128,128]{1,0:T(8,128)S(1)}, f32[128,128]{1,0:T(8,128)S(1)}, u32[]{:S(2)}, u32[]{:S(2)}) collective-permute-start(f32[128,128]{1,0:T(8,128)S(1)} %get-tuple-element.18), channel_id=1, source_target_pairs={{1,0},{2,1},{3,2},{5,4},{6,5},{7,6},{9,8},{10,9},{11,10},{13,12},{... | collective-permute-start | bytes 196616 | tf_op jit(solution)/shard_map/ppermute | solution.py:417
  7.2 0.7 copy-start.2
  13.5 15.1 %all-to-all-start = ((f16[8,96,128]{2,1,0:T(8,128)(2,1)}), f16[8,96,128]{2,1,0:T(8,128)(2,1)S(1)}, u32[]{:S(2)}, u32[]{:S(2)}) async-start(f16[8,96,128]{2,1,0:T(8,128)(2,1)} %convert_element_type.24), calls=%async_computation | async-start | bytes 393216 | tf_op jit(solution)/shard_map/all_to_all | solution.py:402
  22.1 6.6 %collective-permute-start.2 = (f32[8,128]{1,0:T(8,128)S(1)}, f32[8,128]{1,0:T(8,128)S(1)}, u32[]{:S(2)}, u32[]{:S(2)}) collective-permute-start(f32[8,128]{1,0:T(8,128)S(1)} %get-tuple-element.25.t_ref), channel_id=1, source_target_pairs={{0,1},{1,0},{2,3},{3,2},{4,5},{5,4},{6,7},{7,6},{8,9},{9,8},{10,11... | collective-permute-start | bytes 12296 | tf_op jit(solution)/shard_map/ppermute | solution.py:439

commit v5 on v4

--- a/solution.py
+++ b/solution.py
@@ -334,19 +334,27 @@
 def far_kernel(place_ref, r_ref, send_ref, value_ref, matrix_ref):
     count = r_ref.shape[0]
     me = place_ref[0]
-    span = own = (jnp.zeros((64, 64), F32), jnp.zeros((64, 128), F32))
+    spans, traces = [], []
+    for i in range(count):
+        change, value, t = take(r_ref[i])
+        spans.append((change, value))
+        traces.append(t)
+    upto = [(jnp.zeros((64, 64), F32), jnp.zeros((64, 128), F32)), spans[0]]
+    upto.append(join(spans[0], spans[1]))
+    if count == 4:
+        upto.append(join(upto[2], spans[2]))
+        upto.append(join(upto[2], join(spans[2], spans[3])))
+    own = upto[0]
     before = total = mine = jnp.zeros((8, 1), F32)
     for i in range(count):
-        own = tuple(jnp.where(me == i, new, old) for new, old in zip(span, own))
-        change, value, t = take(r_ref[i])
+        own = tuple(jnp.where(me == i, new, old) for new, old in zip(upto[i], own))
         before = jnp.where(me == i, total, before)
-        mine = jnp.where(me == i, t, mine)
-        total = total + t
-        span = join(span, (change, value)) if i else (change, value)
+        mine = jnp.where(me == i, traces[i], mine)
+        total = total + traces[i]
     matrix_ref[...], value_ref[...] = own
     spread = jnp.sum(before, axis=0, keepdims=True)
     t = jnp.concatenate([total[:2], mine[:2], spread, jnp.zeros((3, 1), F32)], axis=0)
-    put(send_ref, *span, jnp.broadcast_to(t, (8, 128)))
+    put(send_ref, *upto[count], jnp.broadcast_to(t, (8, 128)))
 
 
 def back_kernel(
@@ -365,7 +373,7 @@
         total = total + t
         if i < count - 1:
             change, value, _ = take(r_ref[copies * i + strip])
-            state = state + mix(change, state) + value
+            state = state + mix(change, state) + value if i else value
     entry = own + mix(far_matrix[...], own) + far_value[...]
     near = near_matrix.shape[0]
     states = mix(near_matrix[...].reshape(near * 64, 64), entry)
@@ -436,7 +444,10 @@
         20,
     )
     got = exchange(send, NEAR)
-    other = lax.ppermute(trace, "sl", [(0, 1), (1, 0)])
+    across = [(i, i ^ 1) for i in range(strips)]
+    other = lax.ppermute(
+        trace, SPACE, [((i + 1) % strips, (j + 1) % strips) for i, j in across]
+    )
     send, near_value, near_matrix = call(
         near_kernel,
         [(far, 104, 128), (near, 64, 128), (near, 64, 64)],
@@ -454,14 +465,14 @@
         "far",
         8,
     )
-    got = exchange(send, ("x", "sh"))
+    got = exchange(send, ("x", "sl"))
     (send,) = call(
         back_kernel,
         [(near, 72, 128)],
         2,
         (
             lax.axis_index("x").reshape(1),
-            lax.axis_index("sh").reshape(1),
+            lax.axis_index("sl").reshape(1),
             got,
             far_value,
             far_matrix,

time: 84.2 us -> 81.1 us (0.963)
  blocking collectives: 51.1 us -> 48.3 us
    all_to_all x3, blocking collectives: 51.1 us -> 48.3 us  [exchange(): return lax.all_to_all(v.astype(F16), axes, 0, 0, tiled=True).astype(F32)]
where the time goes in v5:
time: 81.1 us; the launch traced here: 80.7 us
  blocking collectives  48.3 us (60%)
  starting transfers between devices  16.3 us (20%)
  Pallas kernels  8.11 us (10%)
  waiting for transfers between devices  5.63 us (7%)
  other arithmetic  0.87 us (1%)
    all_to_all x3, blocking collectives, exchange(): return lax.all_to_all(v.astype(F16), axes, 0, 0, tiled=True).astype(F32)  48.3 us
    all_to_all x1, starting transfers between devices, exchange(): return lax.all_to_all(v.astype(F16), axes, 0, 0, tiled=True).astype(F32)  8.55 us
    pallas_call x6, Pallas kernels, call(): pl.pallas_call(kernel, in_specs=[scalars()] * places + [whole()] * (len(a...  6.94 us
    all_to_all x1, waiting for transfers between devices, exchange(): return lax.all_to_all(v.astype(F16), axes, 0, 0, tiled=True).astype(F32)  4.07 us
    ppermute x1, starting transfers between devices, body(): low = lax.ppermute(down, SPACE, forward)  4.02 us
    ppermute x1, starting transfers between devices, body(): lax.ppermute(trace, SPACE, [((i + 1) % strips, (j + 1) % strips) for i, j...  2.46 us
  transfers between devices with their start and end apart: 4, of which 2 were waited for; matrix products, arithmetic and copies ran while one was open for 0% of the time, Pallas kernels for 2%

profile of v5, /device:TPU:1, one launch (start us, length us, event | category | flops | bytes accessed | tf_op | source)
XLA Modules:
  0.0 80.7 jit_solution(8244983297572169274)
XLA Ops:
  0.6 0.0 copy-start
  0.6 0.0 copy-start.1
  0.6 1.2 %edges.1 = (f32[128,128]{1,0:T(8,128)S(1)}, f32[128,128]{1,0:T(8,128)S(1)}, bf16[2,64,576]{2,1,0:T(8,128)(2,1)S(1)}) custom-call(f32[1,1,64,1024]{3,2,1,0:T(8,128)} %g_ref.7, bf16[2,1,64,1024]{3,2,1,0:T(8,128)(2,1)} %p_ref.5, bf16[2,64,576]{2,1,0:T(8,128)(2,1)} %k_ref.1), custom_call_target="tpu_custom_call" | custom-call | tf_op jit(solution)/shard_map/edges/pallas_call | solution.py:78
  1.8 4.0 %collective-permute-start = (f32[128,128]{1,0:T(8,128)S(1)}, f32[128,128]{1,0:T(8,128)S(1)}, u32[]{:S(2)}, u32[]{:S(2)}) collective-permute-start(f32[128,128]{1,0:T(8,128)S(1)} %get-tuple-element.17), channel_id=1, source_target_pairs={{0,1},{1,2},{2,3},{4,5},{5,6},{6,7},{8,9},{9,10},{10,11},{12,13},{... | collective-permute-start | bytes 196616 | tf_op jit(solution)/shard_map/ppermute | solution.py:424
  5.9 1.3 %collective-permute-start.1 = (f32[128,128]{1,0:T(8,128)S(1)}, f32[128,128]{1,0:T(8,128)S(1)}, u32[]{:S(2)}, u32[]{:S(2)}) collective-permute-start(f32[128,128]{1,0:T(8,128)S(1)} %get-tuple-element.18), channel_id=1, source_target_pairs={{1,0},{2,1},{3,2},{5,4},{6,5},{7,6},{9,8},{10,9},{11,10},{13,12},{... | collective-permute-start | bytes 196616 | tf_op jit(solution)/shard_map/ppermute | solution.py:425
  7.2 0.0 copy-start.2
  7.2 0.0 copy-done
  7.2 0.0 copy-done.1
  7.2 0.7 copy-done.2
  7.9 1.4 %inner.1 = (f32[64,1024]{1,0:T(8,128)S(1)}, f32[64,1024]{1,0:T(8,128)S(1)}, f32[32,128]{1,0:T(8,128)S(1)}, f32[8,128]{1,0:T(8,128)S(1)}) custom-call(s32[1]{0:T(128)} %bitcast.place_ref, f32[1,1,64,1024]{3,2,1,0:T(8,128)S(1)} %copy-done, bf16[2,1,64,1024]{3,2,1,0:T(8,128)(2,1)S(1)} %copy-done.1, bf16[2,64,576]{2,1,0:T(8,128)(2,1)S(1)} %get-tuple-element.19.k_ref, ...), custom_call_target="tpu_custom_call" | custom-call | flops 450000000 | bytes 2000000 | tf_op jit(solution)/shard_map/inner/pallas_call | solution.py:244
  9.3 0.0 collective-permute-done.low_ref
  9.3 1.6 %collective-permute-done.1.high_ref = f32[128,128]{1,0:T(8,128)S(1)} collective-permute-done((f32[128,128]{1,0:T(8,128)S(1)}, f32[128,128]{1,0:T(8,128)S(1)}, u32[]{:S(2)}, u32[]{:S(2)}) %collective-permute-start.1) | collective-permute-done | bytes 65568 | tf_op jit(solution)/shard_map/ppermute | solution.py:425
  10.9 1.9 %outer.1 = (f32[8,96,128]{2,1,0:T(8,128)S(1)}, f32[8,128]{1,0:T(8,128)S(1)}) custom-call(s32[1]{0:T(128)} %bitcast.5.strip_ref, f32[1,1,64,1024]{3,2,1,0:T(8,128)S(1)} %copy-done, f32[128,128]{1,0:T(8,128)S(1)} %collective-permute-done.low_ref, f32[128,128]{1,0:T(8,128)S(1)} %collective-permute-done.1.high_ref, bf16[2,1,64,1024]{3,2,1,0:T(8,128)(2,1)S(1)} %copy-done.1, ...), custom_call_target="tpu_custom_call" | custom-call | tf_op jit(solution)/shard_map/outer/pallas_call | solution.py:244
  12.8 0.7 convert_element_type.24
  13.5 8.6 %all-to-all-start = ((f16[8,96,128]{2,1,0:T(8,128)(2,1)}), f16[8,96,128]{2,1,0:T(8,128)(2,1)S(1)}, u32[]{:S(2)}, u32[]{:S(2)}) async-start(f16[8,96,128]{2,1,0:T(8,128)(2,1)} %convert_element_type.24), calls=%async_computation | async-start | bytes 393216 | tf_op jit(solution)/shard_map/all_to_all | solution.py:410
  22.1 2.5 %collective-permute-start.2 = (f32[8,128]{1,0:T(8,128)S(1)}, f32[8,128]{1,0:T(8,128)S(1)}, u32[]{:S(2)}, u32[]{:S(2)}) collective-permute-start(f32[8,128]{1,0:T(8,128)S(1)} %get-tuple-element.25.t_ref), channel_id=1, source_target_pairs={{1,2},{2,1},{3,0},{0,3},{5,6},{6,5},{7,4},{4,7},{9,10},{10,9},{11,... | collective-permute-start | bytes 12296 | tf_op jit(solution)/shard_map/ppermute | solution.py:448
  24.5 4.1 %all-to-all-done = f16[8,96,128]{2,1,0:T(8,128)(2,1)S(1)} async-done(((f16[8,96,128]{2,1,0:T(8,128)(2,1)}), f16[8,96,128]{2,1,0:T(8,128)(2,1)S(1)}, u32[]{:S(2)}, u32[]{:S(2)}) %all-to-all-start) | async-done | bytes 196640 | tf_op jit(solution)/shard_map/all_to_all | solution.py:410
  28.6 0.0 collective-permute-done.2.other_ref
  28.7 0.9 %near.1 = (f32[4,104,128]{2,1,0:T(8,128)S(1)}, f32[8,64,128]{2,1,0:T(8,128)S(1)}, f32[8,64,64]{2,1,0:T(8,128)S(1)}) custom-call(f32[8,96,128]{2,1,0:T(8,128)S(1)} %convert_element_type.25.r_ref, f32[8,128]{1,0:T(8,128)S(1)} %get-tuple-element.25.t_ref, f32[8,128]{1,0:T(8,128)S(1)} %collective-permute-done.2.other_ref), custom_call_target="tpu_custom_call" | custom-call | tf_op jit(solution)/shard_map/near/pallas_call | solution.py:244
  29.6 23.5 %all_to_all.20 = f16[4,104,128]{2,1,0:T(8,128)(2,1)S(1)} all-to-all(f16[4,104,128]{2,1,0:T(8,128)(2,1)S(1)} %convert_element_type.26), channel_id=1, replica_groups=mesh['x'=4,'zh'=4,'zl'=4,'c'=2,'sh'=2,'sl'=2] {'zh'}, dimensions={0} | all-to-all | bytes 212992 | tf_op jit(solution)/shard_map/all_to_all | solution.py:410
  53.1 0.7 far.1
  53.8 11.4 %all_to_all.21 = f16[8,104,128]{2,1,0:T(8,128)(2,1)S(1)} all-to-all(f16[8,104,128]{2,1,0:T(8,128)(2,1)S(1)} %convert_element_type.28), channel_id=1, replica_groups=mesh['x'=4,'zh'=4,'zl'=4,'c'=2,'sh'=2,'sl'=2] {'x','sl'}, dimensions={0} | all-to-all | bytes 425984 | tf_op jit(solution)/shard_map/all_to_all | solution.py:410
  65.3 1.1 %back.1 = f32[8,72,128]{2,1,0:T(8,128)S(1)} custom-call(s32[1]{0:T(128)} %bitcast.2.place_ref, s32[1]{0:T(128)} %bitcast.3.strip_ref, f32[8,104,128]{2,1,0:T(8,128)S(1)} %convert_element_type.29.r_ref, f32[64,128]{1,0:T(8,128)S(1)} %get-tuple-element.28.far_value, f32[64,64]{1,0:T(8,128)S(1)} %get-tuple-element.29.far_matrix, ...), custom_call_target="tpu_custom_call" | custom-call | tf_op jit(solution)/shard_map/back/pallas_call | solution.py:244
  66.4 13.4 %all_to_all.22 = f16[8,72,128]{2,1,0:T(8,128)(2,1)S(1)} all-to-all(f16[8,72,128]{2,1,0:T(8,128)(2,1)S(1)} %convert_element_type.30), channel_id=1, replica_groups=mesh['x'=4,'zh'=4,'zl'=4,'c'=2,'sh'=2,'sl'=2] {'zl','c'}, dimensions={0} | all-to-all | bytes 294912 | tf_op jit(solution)/shard_map/all_to_all | solution.py:410
  79.8 0.9 %final.1 = (f32[1,1,64,1024]{3,2,1,0:T(8,128)}, f32[2]{0:T(128)}) custom-call(s32[1]{0:T(128)} %bitcast.place_ref, s32[1]{0:T(128)} %bitcast.1.me_ref, f32[8,72,128]{2,1,0:T(8,128)S(1)} %convert_element_type.31.r_ref, f32[1,1,64,1024]{3,2,1,0:T(8,128)S(1)} %copy-done), custom_call_target="tpu_custom_call" | custom-call | tf_op jit(solution)/shard_map/final/pallas_call | solution.py:244
  (7 shorter events, 0.2 us)
Async XLA Ops:
  0.6 6.6 %copy-start = (f32[1,1,64,1024]{3,2,1,0:T(8,128)S(1)}, f32[1,1,64,1024]{3,2,1,0:T(8,128)}, u32[]{:S(2)}) copy-start(f32[1,1,64,1024]{3,2,1,0:T(8,128)} %g_ref.7) | copy-start | bytes 786436
  0.6 6.6 %copy-start.1 = (bf16[2,1,64,1024]{3,2,1,0:T(8,128)(2,1)S(1)}, bf16[2,1,64,1024]{3,2,1,0:T(8,128)(2,1)}, u32[]{:S(2)}) copy-start(bf16[2,1,64,1024]{3,2,1,0:T(8,128)(2,1)} %p_ref.5) | copy-start | bytes 786436
  1.8 7.5 %collective-permute-start = (f32[128,128]{1,0:T(8,128)S(1)}, f32[128,128]{1,0:T(8,128)S(1)}, u32[]{:S(2)}, u32[]{:S(2)}) collective-permute-start(f32[128,128]{1,0:T(8,128)S(1)} %get-tuple-element.17), channel_id=1, source_target_pairs={{0,1},{1,2},{2,3},{4,5},{5,6},{6,7},{8,9},{9,10},{10,11},{12,13},{... | collective-permute-start | bytes 196616 | tf_op jit(solution)/shard_map/ppermute | solution.py:424
  5.9 5.0 %collective-permute-start.1 = (f32[128,128]{1,0:T(8,128)S(1)}, f32[128,128]{1,0:T(8,128)S(1)}, u32[]{:S(2)}, u32[]{:S(2)}) collective-permute-start(f32[128,128]{1,0:T(8,128)S(1)} %get-tuple-element.18), channel_id=1, source_target_pairs={{1,0},{2,1},{3,2},{5,4},{6,5},{7,6},{9,8},{10,9},{11,10},{13,12},{... | collective-permute-start | bytes 196616 | tf_op jit(solution)/shard_map/ppermute | solution.py:425
  7.2 0.7 copy-start.2
  13.5 15.1 %all-to-all-start = ((f16[8,96,128]{2,1,0:T(8,128)(2,1)}), f16[8,96,128]{2,1,0:T(8,128)(2,1)S(1)}, u32[]{:S(2)}, u32[]{:S(2)}) async-start(f16[8,96,128]{2,1,0:T(8,128)(2,1)} %convert_element_type.24), calls=%async_computation | async-start | bytes 393216 | tf_op jit(solution)/shard_map/all_to_all | solution.py:410
  22.1 6.6 %collective-permute-start.2 = (f32[8,128]{1,0:T(8,128)S(1)}, f32[8,128]{1,0:T(8,128)S(1)}, u32[]{:S(2)}, u32[]{:S(2)}) collective-permute-start(f32[8,128]{1,0:T(8,128)S(1)} %get-tuple-element.25.t_ref), channel_id=1, source_target_pairs={{1,2},{2,1},{3,0},{0,3},{5,6},{6,5},{7,4},{4,7},{9,10},{10,9},{11,... | collective-permute-start | bytes 12296 | tf_op jit(solution)/shard_map/ppermute | solution.py:448

commit v6 on v5

--- a/solution.py
+++ b/solution.py
@@ -87,17 +87,23 @@
     )(*held)
 
 
-def taps(v):
+def taps(v, closed=False):
     n = v.shape[1]
     column = lax.broadcasted_iota(jnp.int32, (16, n), 1) & (WIDTH - 1)
     keep = [jnp.where(column == edge, 0.0, 1.0).astype(BF16) for edge in (WIDTH - 1, 0)]
     keep = [jnp.concatenate([k] * (v.shape[0] // 16), axis=0) for k in keep]
     left = pltpu.roll(v * keep[0], 1, 1)
     right = pltpu.roll(v * keep[1], n - 1, 1)
+    lane = lax.broadcasted_iota(jnp.int32, (v.shape[0], 128), 1)
+    low = jnp.where(lane < WIDTH, 1.0, 0.0).astype(BF16)
+    high = jnp.where(lane < WIDTH, 0.0, 1.0).astype(BF16)
     rows = []
     for part in (left, v, right):
         above = pltpu.roll(part, WIDTH, 1)
         below = jnp.concatenate([above[:, 128:], above[:, :128]], axis=1)
+        if closed:
+            above = jnp.concatenate([above[:, :128] * high, above[:, 128:]], axis=1)
+            below = jnp.concatenate([below[:, : n - 128], below[:, n - 128 :] * low], axis=1)
         rows.append((above, part, below))
     return jnp.concatenate([rows[dx][dy] for dy in range(3) for dx in range(3)], axis=0)
 
@@ -117,24 +123,38 @@
     )
 
 
-def side(ref, n):
-    return ref[64:, n * WIDTH : (n + 1) * WIDTH]
-
-
-def inner_kernel(place_ref, g_ref, p_ref, k_ref, b_ref, state_ref, offset_ref, change_ref, t_ref):
+def adjoint(k_ref):
+    blocks = []
+    for at in range(0, 9 * 64, 128):
+        both = jnp.concatenate([k_ref[n, :, at : at + 128].astype(F32) for n in range(2)], axis=0)
+        turned = both.T
+        blocks += [turned[i : i + 64] for i in range(0, turned.shape[0], 64)]
+    blocks = blocks[::-1]
+    return jnp.concatenate(
+        [
+            jnp.concatenate([block[:, n * 64 : (n + 1) * 64] for block in blocks], axis=1)
+            for n in range(2)
+        ],
+        axis=0,
+    ).astype(BF16)
+
+
+def inner_kernel(
+    place_ref, g_ref, p_ref, k_ref, b_ref, state_ref, offset_ref, change_ref, t_ref, pull_ref, a_ref
+):
     leading = place_ref[0] == 0
     g = g_ref[0, 0]
-    cells = g.shape[1]
-    kernel = k_ref[0]
     activation = jnp.tanh(g)
     slopes = 1.0 - activation * activation
-    forcing = STEP * (convolve(kernel, activation) + bias_of(b_ref, 0))
-    total = jnp.zeros((64, cells), F32)
+    forcing = STEP * (convolve(k_ref[0], activation) + bias_of(b_ref, 0))
+    turned = adjoint(k_ref)
+    a_ref[...] = turned
+    total = jnp.zeros(g.shape, F32)
     for n in range(2):
-        probe = p_ref[n, 0].astype(F32)
-        total = total + probe * convolve(kernel, slopes * probe)
-    lane = lax.broadcasted_iota(jnp.int32, (64, cells), 1)
-    total = jnp.where((lane >= WIDTH) & (lane < cells - WIDTH), total, 0.0)
+        probe = p_ref[n, 0]
+        pulled = jnp.dot(turned, taps(probe, True), preferred_element_type=F32)
+        total = total + pulled[:64] * rounded(slopes * probe.astype(F32))
+        pull_ref[n] = pulled[64:]
     t_ref[...] = jnp.full((8, 128), 0.5 * jnp.sum(total))
     both = k_ref[0].astype(F32) + k_ref[1].astype(F32)
     pair = both[:, :128] + both[:, 128:256] + both[:, 256:384] + both[:, 384:512]
@@ -142,6 +162,17 @@
     state_ref[...] = g + forcing
     offset_ref[...] = forcing + jnp.where(leading, g, -mix(coarse, g))
     change_ref[...] = fold(jnp.where(leading, -eye(64), coarse))
+
+
+def sides(v):
+    column = lax.broadcasted_iota(jnp.int32, v.shape, 1) & (WIDTH - 1)
+    left = pltpu.roll(jnp.where(column == WIDTH - 1, 0.0, v), 1, 1)
+    right = pltpu.roll(jnp.where(column == 0, 0.0, v), v.shape[1] - 1, 1)
+    return jnp.concatenate([left, v, right], axis=0).astype(BF16)
+
+
+def twice(v, at):
+    return jnp.concatenate([v[:, at : at + WIDTH]] * 2, axis=1)
 
 
 def outer_kernel(
@@ -157,42 +188,33 @@
     offset_ref,
     change_ref,
     inner_ref,
+    pull_ref,
+    a_ref,
     send_ref,
     t_ref,
 ):
     cells = state_ref.shape[1]
     last = cells - 128
-    zero = jnp.zeros((64, WIDTH), F32)
     ends = jnp.concatenate(
         [low_ref[:64], g_ref[0, 0, :, :128], g_ref[0, 0, :, last:], high_ref[:64]], axis=1
     )
     probe_mid = [p_ref[n, 0].astype(F32) for n in range(2)]
     activation = jnp.tanh(ends)
-    slopes = 1.0 - activation * activation
-    kernel = k_ref[0]
-    forcing = STEP * (convolve(kernel, activation) + bias_of(b_ref, 0))
-    total = jnp.zeros((64, 128), F32)
-    for n in range(2):
-        probe = jnp.concatenate(
-            [
-                zero,
-                side(low_ref, n),
-                probe_mid[n][:, :128],
-                probe_mid[n][:, last:],
-                side(high_ref, n),
-                zero,
-            ],
-            axis=1,
-        )
-        found = convolve(kernel, slopes * probe, slice(128, 384))
-        total = total + jnp.concatenate(
-            [
-                probe_mid[n][:, :WIDTH] * found[:, :WIDTH],
-                probe_mid[n][:, last + WIDTH :] * found[:, 256 - WIDTH :],
-            ],
-            axis=1,
-        )
-    rows = lax.broadcasted_iota(jnp.int32, (8, 128), 0)
+    end_slopes = 1.0 - activation * activation
+    forcing = STEP * (convolve(k_ref[0], activation) + bias_of(b_ref, 0))
+
+    turned = a_ref[...]
+    pulls = [
+        jnp.dot(turned[:, :192], sides(low_ref[64:]), preferred_element_type=F32),
+        jnp.dot(turned[:, 384:], sides(high_ref[64:]), preferred_element_type=F32),
+    ]
+    edge_probe = [
+        jnp.concatenate([v[:, :WIDTH] for v in probe_mid], axis=1),
+        jnp.concatenate([v[:, cells - WIDTH :] for v in probe_mid], axis=1),
+    ]
+    total = sum(
+        pulls[i][:64] * rounded(twice(end_slopes, (128, 320)[i]) * edge_probe[i]) for i in range(2)
+    )
     trace = inner_ref[...] + 0.5 * jnp.sum(total)
 
     lane = lax.broadcasted_iota(jnp.int32, (64, 128), 1)
@@ -208,19 +230,19 @@
     outside = ((strip_ref[0] == 0) & (far_lane < 128)) | (
         (strip_ref[0] == strips - 1) & (far_lane >= wide - 128)
     )
-    middle = slice(128, 128 + cells)
     activation = jnp.where(outside, 0.0, jnp.tanh(current))
-    slopes = 1.0 - activation * activation
-    kernel = k_ref[1]
-    forcing = STEP * (convolve(kernel, activation, middle) + bias_of(b_ref, 1))
-    total = jnp.zeros((64, cells), F32)
-    for n in range(2):
-        probe = jnp.concatenate(
-            [zero, side(low_ref, n), probe_mid[n], side(high_ref, n), zero], axis=1
-        )
-        total = total + probe_mid[n] * convolve(kernel, slopes * probe, middle)
-    trace = jnp.where(rows == 1, 0.5 * jnp.sum(total), jnp.where(rows == 0, trace, 0.0))
-    t_ref[...] = trace
+    forcing = convolve(k_ref[1], activation, slice(128, 128 + cells))
+    forcing = STEP * (forcing + bias_of(b_ref, 1))
+    middle = activation[:, 128 : 128 + cells]
+    slopes = 1.0 - middle * middle
+    total = sum(pull_ref[n] * rounded(slopes * probe_mid[n]) for n in range(2))
+    edge = sum(
+        pulls[i][64:] * rounded(twice(slopes, (0, cells - WIDTH)[i]) * edge_probe[i])
+        for i in range(2)
+    )
+    rows = lax.broadcasted_iota(jnp.int32, (8, 128), 0)
+    second = 0.5 * (jnp.sum(total) + jnp.sum(edge))
+    t_ref[...] = jnp.where(rows == 1, second, jnp.where(rows == 0, trace, 0.0))
     for j in range(cells // 128):
         at = slice(j * 128, (j + 1) * 128)
         part = offset_ref[:, at] + forcing[:, at]
@@ -240,12 +262,16 @@
     return pl.BlockSpec(memory_space=pltpu.SMEM)
 
 
+def extent(shape):
+    return getattr(shape, "shape", shape)
+
+
 def call(kernel, shapes, places, args, name, room, cost=None):
     return pl.pallas_call(
         kernel,
         in_specs=[scalars()] * places + [whole()] * (len(args) - places),
-        out_specs=[whole() if len(s) > 1 else scalars() for s in shapes],
-        out_shape=[jax.ShapeDtypeStruct(s, F32) for s in shapes],
+        out_specs=[whole() if len(s) > 1 else scalars() for s in map(extent, shapes)],
+        out_shape=[s if hasattr(s, "dtype") else jax.ShapeDtypeStruct(s, F32) for s in shapes],
         compiler_params=pltpu.CompilerParams(vmem_limit_bytes=room << 20),
         cost_estimate=cost,
         name=name,
@@ -423,9 +449,16 @@
     backward = [(i + 1, i) for i in range(strips - 1)]
     low = lax.ppermute(down, SPACE, forward)
     high = lax.ppermute(up, SPACE, backward)
-    state, offset, change, inner = call(
+    state, offset, change, inner, pull, turned = call(
         inner_kernel,
-        [(64, cells), (64, cells), (32, 128), (8, 128)],
+        [
+            (64, cells),
+            (64, cells),
+            (32, 128),
+            (8, 128),
+            (2, 64, cells),
+            jax.ShapeDtypeStruct((128, 576), BF16),
+        ],
         1,
         (place, guess, probes, kernels, biases),
         "inner",
@@ -438,7 +471,7 @@
         1,
         (
             strip.reshape(1), guess, low, high, probes, kernels, biases,
-            state, offset, change, inner,
+            state, offset, change, inner, pull, turned,
         ),
         "outer",
         20,

time: 81.1 us -> 80.1 us (0.988)
  Pallas kernels: 8.11 us -> 7.29 us
    pallas_call x6, Pallas kernels: 6.94 us -> 6.12 us  [call(): pl.pallas_call(kernel, in_specs=[scalars()] * places + [whole()] * (len(a...]
where the time goes in v6:
time: 80.1 us; the launch traced here: 79.7 us
  blocking collectives  48.3 us (60%)
  starting transfers between devices  16.5 us (21%)
  Pallas kernels  7.29 us (9%)
  waiting for transfers between devices  5.35 us (7%)
  other arithmetic  0.87 us (1%)
  between operations  0.81 us (1%)
    all_to_all x3, blocking collectives, exchange(): return lax.all_to_all(v.astype(F16), axes, 0, 0, tiled=True).astype(F32)  48.3 us
    all_to_all x1, starting transfers between devices, exchange(): return lax.all_to_all(v.astype(F16), axes, 0, 0, tiled=True).astype(F32)  8.55 us
    pallas_call x6, Pallas kernels, call(): pl.pallas_call(kernel, in_specs=[scalars()] * places + [whole()] * (len(a...  6.12 us
    ppermute x1, starting transfers between devices, body(): low = lax.ppermute(down, SPACE, forward)  4.02 us
    all_to_all x1, waiting for transfers between devices, exchange(): return lax.all_to_all(v.astype(F16), axes, 0, 0, tiled=True).astype(F32)  3.93 us
    ppermute x1, starting transfers between devices, body(): lax.ppermute(trace, SPACE, [((i + 1) % strips, (j + 1) % strips) for i, j...  2.6 us
  transfers between devices with their start and end apart: 4, of which 2 were waited for; matrix products, arithmetic and copies ran while one was open for 0% of the time, Pallas kernels for 2%

profile of v6, /device:TPU:1, one launch (start us, length us, event | category | flops | bytes accessed | tf_op | source)
XLA Modules:
  0.0 79.7 jit_solution(14924582613905179887)
XLA Ops:
  0.6 0.0 copy-start
  0.6 0.0 copy-start.1
  0.6 1.2 %edges.1 = (f32[128,128]{1,0:T(8,128)S(1)}, f32[128,128]{1,0:T(8,128)S(1)}, bf16[2,64,576]{2,1,0:T(8,128)(2,1)S(1)}) custom-call(f32[1,1,64,1024]{3,2,1,0:T(8,128)} %g_ref.7, bf16[2,1,64,1024]{3,2,1,0:T(8,128)(2,1)} %p_ref.5, bf16[2,64,576]{2,1,0:T(8,128)(2,1)} %k_ref.1), custom_call_target="tpu_custom_call" | custom-call | tf_op jit(solution)/shard_map/edges/pallas_call | solution.py:78
  1.8 4.0 %collective-permute-start = (f32[128,128]{1,0:T(8,128)S(1)}, f32[128,128]{1,0:T(8,128)S(1)}, u32[]{:S(2)}, u32[]{:S(2)}) collective-permute-start(f32[128,128]{1,0:T(8,128)S(1)} %get-tuple-element.19), channel_id=1, source_target_pairs={{0,1},{1,2},{2,3},{4,5},{5,6},{6,7},{8,9},{9,10},{10,11},{12,13},{... | collective-permute-start | bytes 196616 | tf_op jit(solution)/shard_map/ppermute | solution.py:450
  5.9 1.3 %collective-permute-start.1 = (f32[128,128]{1,0:T(8,128)S(1)}, f32[128,128]{1,0:T(8,128)S(1)}, u32[]{:S(2)}, u32[]{:S(2)}) collective-permute-start(f32[128,128]{1,0:T(8,128)S(1)} %get-tuple-element.20), channel_id=1, source_target_pairs={{1,0},{2,1},{3,2},{5,4},{6,5},{7,6},{9,8},{10,9},{11,10},{13,12},{... | collective-permute-start | bytes 196616 | tf_op jit(solution)/shard_map/ppermute | solution.py:451
  7.2 0.0 copy-start.2
  7.2 0.0 copy-done
  7.2 0.0 copy-done.1
  7.2 0.7 copy-done.2
  7.9 1.6 %inner.1 = (f32[64,1024]{1,0:T(8,128)S(1)}, f32[64,1024]{1,0:T(8,128)S(1)}, f32[32,128]{1,0:T(8,128)S(1)}, f32[8,128]{1,0:T(8,128)S(1)}, f32[2,64,1024]{2,1,0:T(8,128)S(1)}, /*index=5*/bf16[128,576]{1,0:T(8,128)(2,1)S(1)}) custom-call(s32[1]{0:T(128)} %bitcast.place_ref, f32[1,1,64,1024]{3,2,1,0:T(8,128)S(1)} %copy-done, ...), custom_call_target="tpu_custom_call" | custom-call | flops 450000000 | bytes 2000000 | tf_op jit(solution)/shard_map/inner/pallas_call | solution.py:270
  9.4 0.0 collective-permute-done.low_ref
  9.5 1.4 %collective-permute-done.1.high_ref = f32[128,128]{1,0:T(8,128)S(1)} collective-permute-done((f32[128,128]{1,0:T(8,128)S(1)}, f32[128,128]{1,0:T(8,128)S(1)}, u32[]{:S(2)}, u32[]{:S(2)}) %collective-permute-start.1) | collective-permute-done | bytes 65568 | tf_op jit(solution)/shard_map/ppermute | solution.py:451
  10.9 1.0 %outer.1 = (f32[8,96,128]{2,1,0:T(8,128)S(1)}, f32[8,128]{1,0:T(8,128)S(1)}) custom-call(s32[1]{0:T(128)} %bitcast.5.strip_ref, f32[1,1,64,1024]{3,2,1,0:T(8,128)S(1)} %copy-done, f32[128,128]{1,0:T(8,128)S(1)} %collective-permute-done.low_ref, f32[128,128]{1,0:T(8,128)S(1)} %collective-permute-done.1.high_ref, bf16[2,1,64,1024]{3,2,1,0:T(8,128)(2,1)S(1)} %copy-done.1, ...), custom_call_target="tpu_custom_call" | custom-call | tf_op jit(solution)/shard_map/outer/pallas_call | solution.py:270
  11.9 0.7 convert_element_type.24
  12.6 8.6 %all-to-all-start = ((f16[8,96,128]{2,1,0:T(8,128)(2,1)}), f16[8,96,128]{2,1,0:T(8,128)(2,1)S(1)}, u32[]{:S(2)}, u32[]{:S(2)}) async-start(f16[8,96,128]{2,1,0:T(8,128)(2,1)} %convert_element_type.24), calls=%async_computation | async-start | bytes 393216 | tf_op jit(solution)/shard_map/all_to_all | solution.py:436
  21.1 2.6 %collective-permute-start.2 = (f32[8,128]{1,0:T(8,128)S(1)}, f32[8,128]{1,0:T(8,128)S(1)}, u32[]{:S(2)}, u32[]{:S(2)}) collective-permute-start(f32[8,128]{1,0:T(8,128)S(1)} %get-tuple-element.29.t_ref), channel_id=1, source_target_pairs={{1,2},{2,1},{3,0},{0,3},{5,6},{6,5},{7,4},{4,7},{9,10},{10,9},{11,... | collective-permute-start | bytes 12296 | tf_op jit(solution)/shard_map/ppermute | solution.py:481
  23.7 3.9 %all-to-all-done = f16[8,96,128]{2,1,0:T(8,128)(2,1)S(1)} async-done(((f16[8,96,128]{2,1,0:T(8,128)(2,1)}), f16[8,96,128]{2,1,0:T(8,128)(2,1)S(1)}, u32[]{:S(2)}, u32[]{:S(2)}) %all-to-all-start) | async-done | bytes 196640 | tf_op jit(solution)/shard_map/all_to_all | solution.py:436
  27.7 0.0 collective-permute-done.2.other_ref
  27.7 0.9 %near.1 = (f32[4,104,128]{2,1,0:T(8,128)S(1)}, f32[8,64,128]{2,1,0:T(8,128)S(1)}, f32[8,64,64]{2,1,0:T(8,128)S(1)}) custom-call(f32[8,96,128]{2,1,0:T(8,128)S(1)} %convert_element_type.25.r_ref, f32[8,128]{1,0:T(8,128)S(1)} %get-tuple-element.29.t_ref, f32[8,128]{1,0:T(8,128)S(1)} %collective-permute-done.2.other_ref), custom_call_target="tpu_custom_call" | custom-call | tf_op jit(solution)/shard_map/near/pallas_call | solution.py:270
  28.6 23.5 %all_to_all.20 = f16[4,104,128]{2,1,0:T(8,128)(2,1)S(1)} all-to-all(f16[4,104,128]{2,1,0:T(8,128)(2,1)S(1)} %convert_element_type.26), channel_id=1, replica_groups=mesh['x'=4,'zh'=4,'zl'=4,'c'=2,'sh'=2,'sl'=2] {'zh'}, dimensions={0} | all-to-all | bytes 212992 | tf_op jit(solution)/shard_map/all_to_all | solution.py:436
  52.1 0.7 far.1
  52.9 11.4 %all_to_all.21 = f16[8,104,128]{2,1,0:T(8,128)(2,1)S(1)} all-to-all(f16[8,104,128]{2,1,0:T(8,128)(2,1)S(1)} %convert_element_type.28), channel_id=1, replica_groups=mesh['x'=4,'zh'=4,'zl'=4,'c'=2,'sh'=2,'sl'=2] {'x','sl'}, dimensions={0} | all-to-all | bytes 425984 | tf_op jit(solution)/shard_map/all_to_all | solution.py:436
  64.3 1.1 %back.1 = f32[8,72,128]{2,1,0:T(8,128)S(1)} custom-call(s32[1]{0:T(128)} %bitcast.2.place_ref, s32[1]{0:T(128)} %bitcast.3.strip_ref, f32[8,104,128]{2,1,0:T(8,128)S(1)} %convert_element_type.29.r_ref, f32[64,128]{1,0:T(8,128)S(1)} %get-tuple-element.32.far_value, f32[64,64]{1,0:T(8,128)S(1)} %get-tuple-element.33.far_matrix, ...), custom_call_target="tpu_custom_call" | custom-call | tf_op jit(solution)/shard_map/back/pallas_call | solution.py:270
  65.4 13.4 %all_to_all.22 = f16[8,72,128]{2,1,0:T(8,128)(2,1)S(1)} all-to-all(f16[8,72,128]{2,1,0:T(8,128)(2,1)S(1)} %convert_element_type.30), channel_id=1, replica_groups=mesh['x'=4,'zh'=4,'zl'=4,'c'=2,'sh'=2,'sl'=2] {'zl','c'}, dimensions={0} | all-to-all | bytes 294912 | tf_op jit(solution)/shard_map/all_to_all | solution.py:436
  78.9 0.9 %final.1 = (f32[1,1,64,1024]{3,2,1,0:T(8,128)}, f32[2]{0:T(128)}) custom-call(s32[1]{0:T(128)} %bitcast.place_ref, s32[1]{0:T(128)} %bitcast.1.me_ref, f32[8,72,128]{2,1,0:T(8,128)S(1)} %convert_element_type.31.r_ref, f32[1,1,64,1024]{3,2,1,0:T(8,128)S(1)} %copy-done), custom_call_target="tpu_custom_call" | custom-call | tf_op jit(solution)/shard_map/final/pallas_call | solution.py:270
  (7 shorter events, 0.2 us)
Async XLA Ops:
  0.6 6.6 %copy-start = (f32[1,1,64,1024]{3,2,1,0:T(8,128)S(1)}, f32[1,1,64,1024]{3,2,1,0:T(8,128)}, u32[]{:S(2)}) copy-start(f32[1,1,64,1024]{3,2,1,0:T(8,128)} %g_ref.7) | copy-start | bytes 786436
  0.6 6.6 %copy-start.1 = (bf16[2,1,64,1024]{3,2,1,0:T(8,128)(2,1)S(1)}, bf16[2,1,64,1024]{3,2,1,0:T(8,128)(2,1)}, u32[]{:S(2)}) copy-start(bf16[2,1,64,1024]{3,2,1,0:T(8,128)(2,1)} %p_ref.5) | copy-start | bytes 786436
  1.8 7.6 %collective-permute-start = (f32[128,128]{1,0:T(8,128)S(1)}, f32[128,128]{1,0:T(8,128)S(1)}, u32[]{:S(2)}, u32[]{:S(2)}) collective-permute-start(f32[128,128]{1,0:T(8,128)S(1)} %get-tuple-element.19), channel_id=1, source_target_pairs={{0,1},{1,2},{2,3},{4,5},{5,6},{6,7},{8,9},{9,10},{10,11},{12,13},{... | collective-permute-start | bytes 196616 | tf_op jit(solution)/shard_map/ppermute | solution.py:450
  5.9 5.0 %collective-permute-start.1 = (f32[128,128]{1,0:T(8,128)S(1)}, f32[128,128]{1,0:T(8,128)S(1)}, u32[]{:S(2)}, u32[]{:S(2)}) collective-permute-start(f32[128,128]{1,0:T(8,128)S(1)} %get-tuple-element.20), channel_id=1, source_target_pairs={{1,0},{2,1},{3,2},{5,4},{6,5},{7,6},{9,8},{10,9},{11,10},{13,12},{... | collective-permute-start | bytes 196616 | tf_op jit(solution)/shard_map/ppermute | solution.py:451
  7.2 0.7 copy-start.2
  12.6 15.1 %all-to-all-start = ((f16[8,96,128]{2,1,0:T(8,128)(2,1)}), f16[8,96,128]{2,1,0:T(8,128)(2,1)S(1)}, u32[]{:S(2)}, u32[]{:S(2)}) async-start(f16[8,96,128]{2,1,0:T(8,128)(2,1)} %convert_element_type.24), calls=%async_computation | async-start | bytes 393216 | tf_op jit(solution)/shard_map/all_to_all | solution.py:436
  21.1 6.6 %collective-permute-start.2 = (f32[8,128]{1,0:T(8,128)S(1)}, f32[8,128]{1,0:T(8,128)S(1)}, u32[]{:S(2)}, u32[]{:S(2)}) collective-permute-start(f32[8,128]{1,0:T(8,128)S(1)} %get-tuple-element.29.t_ref), channel_id=1, source_target_pairs={{1,2},{2,1},{3,0},{0,3},{5,6},{6,5},{7,4},{4,7},{9,10},{10,9},{11,... | collective-permute-start | bytes 12296 | tf_op jit(solution)/shard_map/ppermute | solution.py:481

commit v7 on v6

--- a/solution.py
+++ b/solution.py
@@ -55,7 +55,9 @@
     ).astype(F32)
 
 
-def edge_kernel(g_ref, p_ref, k_ref, up_ref, down_ref, kv_ref, p_first, p_last, sems):
+def edge_kernel(
+    g_ref, p_ref, k_ref, b_ref, up_ref, down_ref, kv_ref, bv_ref, p_first, p_last, sems
+):
     end = g_ref.shape[3] - 128
     first, last = pl.ds(0, 128), pl.ds(end, 128)
     copies = [
@@ -64,6 +66,7 @@
         pltpu.make_async_copy(g_ref.at[0, 0, :, first], up_ref.at[pl.ds(0, 64)], sems.at[2]),
         pltpu.make_async_copy(g_ref.at[0, 0, :, last], down_ref.at[pl.ds(0, 64)], sems.at[3]),
         pltpu.make_async_copy(k_ref, kv_ref, sems.at[4]),
+        pltpu.make_async_copy(b_ref, bv_ref, sems.at[5]),
     ]
     for copy in copies:
         copy.start()
@@ -73,15 +76,15 @@
     down_ref[64:] = jnp.concatenate([p_last[n].astype(F32)[:, WIDTH:] for n in range(2)], axis=1)
 
 
-def edges(guess, probes, kernels):
-    held = [pltpu.with_memory_space_constraint(v, pltpu.HBM) for v in (guess, probes, kernels)]
+def edges(*args):
+    held = [pltpu.with_memory_space_constraint(v, pltpu.HBM) for v in args]
     return pl.pallas_call(
         edge_kernel,
-        in_specs=[pl.BlockSpec(memory_space=pltpu.HBM)] * 3,
-        out_specs=[whole()] * 3,
+        in_specs=[pl.BlockSpec(memory_space=pltpu.HBM)] * 4,
+        out_specs=[whole()] * 4,
         out_shape=[jax.ShapeDtypeStruct((128, 128), F32)] * 2
-        + [jax.ShapeDtypeStruct(kernels.shape, BF16)],
-        scratch_shapes=[pltpu.VMEM((2, 64, 128), BF16)] * 2 + [pltpu.SemaphoreType.DMA((5,))],
+        + [jax.ShapeDtypeStruct(v.shape, v.dtype) for v in args[2:]],
+        scratch_shapes=[pltpu.VMEM((2, 64, 128), BF16)] * 2 + [pltpu.SemaphoreType.DMA((6,))],
         compiler_params=pltpu.CompilerParams(vmem_limit_bytes=2 << 20),
         name="edges",
     )(*held)
@@ -444,7 +447,7 @@
     cells = guess.shape[3]
     place = lax.axis_index(TM).reshape(1)
 
-    up, down, kernels = edges(guess, probes, kernels)
+    up, down, kernels, biases = edges(guess, probes, kernels, biases)
     forward = [(i, i + 1) for i in range(strips - 1)]
     backward = [(i + 1, i) for i in range(strips - 1)]
     low = lax.ppermute(down, SPACE, forward)

time: 80.1 us -> 80.1 us (level)
  waiting for transfers between devices: 5.35 us -> 6.44 us
where the time goes in v7:
time: 80.1 us; the launch traced here: 79.7 us
  blocking collectives  48.3 us (60%)
  starting transfers between devices  16 us (20%)
  Pallas kernels  7.3 us (9%)
  waiting for transfers between devices  6.44 us (8%)
  other arithmetic  0.87 us (1%)
    all_to_all x3, blocking collectives, exchange(): return lax.all_to_all(v.astype(F16), axes, 0, 0, tiled=True).astype(F32)  48.3 us
    all_to_all x1, starting transfers between devices, exchange(): return lax.all_to_all(v.astype(F16), axes, 0, 0, tiled=True).astype(F32)  8.55 us
    pallas_call x6, Pallas kernels, call(): pl.pallas_call(kernel, in_specs=[scalars()] * places + [whole()] * (len(a...  6.12 us
    all_to_all x1, waiting for transfers between devices, exchange(): return lax.all_to_all(v.astype(F16), axes, 0, 0, tiled=True).astype(F32)  4.36 us
    ppermute x1, starting transfers between devices, body(): low = lax.ppermute(down, SPACE, forward)  4.02 us
    ppermute x1, starting transfers between devices, body(): lax.ppermute(trace, SPACE, [((i + 1) % strips, (j + 1) % strips) for i, j...  2.17 us
    ppermute x1, waiting for transfers between devices, body(): high = lax.ppermute(up, SPACE, backward)  2.07 us
  transfers between devices with their start and end apart: 4, of which 2 were waited for; matrix products, arithmetic and copies ran while one was open for 0% of the time, Pallas kernels for 2%

profile of v7, /device:TPU:1, one launch (start us, length us, event | category | flops | bytes accessed | tf_op | source)
XLA Modules:
  0.0 79.7 jit_solution(2071270875837018746)
XLA Ops:
  0.6 0.0 copy-start
  0.6 0.0 copy-start.1
  0.7 1.2 %edges.1 = (f32[128,128]{1,0:T(8,128)S(1)}, f32[128,128]{1,0:T(8,128)S(1)}, bf16[2,64,576]{2,1,0:T(8,128)(2,1)S(1)}, f32[2,64]{1,0:T(2,128)S(1)}) custom-call(f32[1,1,64,1024]{3,2,1,0:T(8,128)} %g_ref.7, bf16[2,1,64,1024]{3,2,1,0:T(8,128)(2,1)} %p_ref.5, bf16[2,64,576]{2,1,0:T(8,128)(2,1)} %k_ref.1, f32[2,64]{1,0:T(2,128)} %b_ref.1), custom_call_target="tpu_custom_call" | custom-call | tf_op jit(solution)/shard_map/edges/pallas_call | solution.py:81
  1.8 4.0 %collective-permute-start = (f32[128,128]{1,0:T(8,128)S(1)}, f32[128,128]{1,0:T(8,128)S(1)}, u32[]{:S(2)}, u32[]{:S(2)}) collective-permute-start(f32[128,128]{1,0:T(8,128)S(1)} %get-tuple-element.20), channel_id=1, source_target_pairs={{0,1},{1,2},{2,3},{4,5},{5,6},{6,7},{8,9},{9,10},{10,11},{12,13},{... | collective-permute-start | bytes 196616 | tf_op jit(solution)/shard_map/ppermute | solution.py:453
  5.9 1.3 %collective-permute-start.1 = (f32[128,128]{1,0:T(8,128)S(1)}, f32[128,128]{1,0:T(8,128)S(1)}, u32[]{:S(2)}, u32[]{:S(2)}) collective-permute-start(f32[128,128]{1,0:T(8,128)S(1)} %get-tuple-element.21), channel_id=1, source_target_pairs={{1,0},{2,1},{3,2},{5,4},{6,5},{7,6},{9,8},{10,9},{11,10},{13,12},{... | collective-permute-start | bytes 196616 | tf_op jit(solution)/shard_map/ppermute | solution.py:454
  7.2 0.0 copy-done
  7.2 0.0 copy-done.1
  7.2 1.6 %inner.1 = (f32[64,1024]{1,0:T(8,128)S(1)}, f32[64,1024]{1,0:T(8,128)S(1)}, f32[32,128]{1,0:T(8,128)S(1)}, f32[8,128]{1,0:T(8,128)S(1)}, f32[2,64,1024]{2,1,0:T(8,128)S(1)}, /*index=5*/bf16[128,576]{1,0:T(8,128)(2,1)S(1)}) custom-call(s32[1]{0:T(128)} %bitcast.place_ref, f32[1,1,64,1024]{3,2,1,0:T(8,128)S(1)} %copy-done, ...), custom_call_target="tpu_custom_call" | custom-call | flops 450000000 | bytes 2000000 | tf_op jit(solution)/shard_map/inner/pallas_call | solution.py:273
  8.8 0.0 collective-permute-done.low_ref
  8.8 2.1 %collective-permute-done.1.high_ref = f32[128,128]{1,0:T(8,128)S(1)} collective-permute-done((f32[128,128]{1,0:T(8,128)S(1)}, f32[128,128]{1,0:T(8,128)S(1)}, u32[]{:S(2)}, u32[]{:S(2)}) %collective-permute-start.1) | collective-permute-done | bytes 65568 | tf_op jit(solution)/shard_map/ppermute | solution.py:454
  10.9 1.0 %outer.1 = (f32[8,96,128]{2,1,0:T(8,128)S(1)}, f32[8,128]{1,0:T(8,128)S(1)}) custom-call(s32[1]{0:T(128)} %bitcast.5.strip_ref, f32[1,1,64,1024]{3,2,1,0:T(8,128)S(1)} %copy-done, f32[128,128]{1,0:T(8,128)S(1)} %collective-permute-done.low_ref, f32[128,128]{1,0:T(8,128)S(1)} %collective-permute-done.1.high_ref, bf16[2,1,64,1024]{3,2,1,0:T(8,128)(2,1)S(1)} %copy-done.1, ...), custom_call_target="tpu_custom_call" | custom-call | tf_op jit(solution)/shard_map/outer/pallas_call | solution.py:273
  11.9 0.7 convert_element_type.24
  12.6 8.6 %all-to-all-start = ((f16[8,96,128]{2,1,0:T(8,128)(2,1)}), f16[8,96,128]{2,1,0:T(8,128)(2,1)S(1)}, u32[]{:S(2)}, u32[]{:S(2)}) async-start(f16[8,96,128]{2,1,0:T(8,128)(2,1)} %convert_element_type.24), calls=%async_computation | async-start | bytes 393216 | tf_op jit(solution)/shard_map/all_to_all | solution.py:439
  21.1 2.2 %collective-permute-start.2 = (f32[8,128]{1,0:T(8,128)S(1)}, f32[8,128]{1,0:T(8,128)S(1)}, u32[]{:S(2)}, u32[]{:S(2)}) collective-permute-start(f32[8,128]{1,0:T(8,128)S(1)} %get-tuple-element.31.t_ref), channel_id=1, source_target_pairs={{1,2},{2,1},{3,0},{0,3},{5,6},{6,5},{7,4},{4,7},{9,10},{10,9},{11,... | collective-permute-start | bytes 12296 | tf_op jit(solution)/shard_map/ppermute | solution.py:484
  23.3 4.4 %all-to-all-done = f16[8,96,128]{2,1,0:T(8,128)(2,1)S(1)} async-done(((f16[8,96,128]{2,1,0:T(8,128)(2,1)}), f16[8,96,128]{2,1,0:T(8,128)(2,1)S(1)}, u32[]{:S(2)}, u32[]{:S(2)}) %all-to-all-start) | async-done | bytes 196640 | tf_op jit(solution)/shard_map/all_to_all | solution.py:439
  27.7 0.0 collective-permute-done.2.other_ref
  27.7 0.9 %near.1 = (f32[4,104,128]{2,1,0:T(8,128)S(1)}, f32[8,64,128]{2,1,0:T(8,128)S(1)}, f32[8,64,64]{2,1,0:T(8,128)S(1)}) custom-call(f32[8,96,128]{2,1,0:T(8,128)S(1)} %convert_element_type.25.r_ref, f32[8,128]{1,0:T(8,128)S(1)} %get-tuple-element.31.t_ref, f32[8,128]{1,0:T(8,128)S(1)} %collective-permute-done.2.other_ref), custom_call_target="tpu_custom_call" | custom-call | tf_op jit(solution)/shard_map/near/pallas_call | solution.py:273
  28.6 23.5 %all_to_all.20 = f16[4,104,128]{2,1,0:T(8,128)(2,1)S(1)} all-to-all(f16[4,104,128]{2,1,0:T(8,128)(2,1)S(1)} %convert_element_type.26), channel_id=1, replica_groups=mesh['x'=4,'zh'=4,'zl'=4,'c'=2,'sh'=2,'sl'=2] {'zh'}, dimensions={0} | all-to-all | bytes 212992 | tf_op jit(solution)/shard_map/all_to_all | solution.py:439
  52.1 0.7 far.1
  52.9 11.4 %all_to_all.21 = f16[8,104,128]{2,1,0:T(8,128)(2,1)S(1)} all-to-all(f16[8,104,128]{2,1,0:T(8,128)(2,1)S(1)} %convert_element_type.28), channel_id=1, replica_groups=mesh['x'=4,'zh'=4,'zl'=4,'c'=2,'sh'=2,'sl'=2] {'x','sl'}, dimensions={0} | all-to-all | bytes 425984 | tf_op jit(solution)/shard_map/all_to_all | solution.py:439
  64.3 1.1 %back.1 = f32[8,72,128]{2,1,0:T(8,128)S(1)} custom-call(s32[1]{0:T(128)} %bitcast.2.place_ref, s32[1]{0:T(128)} %bitcast.3.strip_ref, f32[8,104,128]{2,1,0:T(8,128)S(1)} %convert_element_type.29.r_ref, f32[64,128]{1,0:T(8,128)S(1)} %get-tuple-element.34.far_value, f32[64,64]{1,0:T(8,128)S(1)} %get-tuple-element.35.far_matrix, ...), custom_call_target="tpu_custom_call" | custom-call | tf_op jit(solution)/shard_map/back/pallas_call | solution.py:273
  65.5 13.4 %all_to_all.22 = f16[8,72,128]{2,1,0:T(8,128)(2,1)S(1)} all-to-all(f16[8,72,128]{2,1,0:T(8,128)(2,1)S(1)} %convert_element_type.30), channel_id=1, replica_groups=mesh['x'=4,'zh'=4,'zl'=4,'c'=2,'sh'=2,'sl'=2] {'zl','c'}, dimensions={0} | all-to-all | bytes 294912 | tf_op jit(solution)/shard_map/all_to_all | solution.py:439
  78.9 0.9 %final.1 = (f32[1,1,64,1024]{3,2,1,0:T(8,128)}, f32[2]{0:T(128)}) custom-call(s32[1]{0:T(128)} %bitcast.place_ref, s32[1]{0:T(128)} %bitcast.1.me_ref, f32[8,72,128]{2,1,0:T(8,128)S(1)} %convert_element_type.31.r_ref, f32[1,1,64,1024]{3,2,1,0:T(8,128)S(1)} %copy-done), custom_call_target="tpu_custom_call" | custom-call | tf_op jit(solution)/shard_map/final/pallas_call | solution.py:273
  (7 shorter events, 0.2 us)
Async XLA Ops:
  0.6 6.6 %copy-start = (f32[1,1,64,1024]{3,2,1,0:T(8,128)S(1)}, f32[1,1,64,1024]{3,2,1,0:T(8,128)}, u32[]{:S(2)}) copy-start(f32[1,1,64,1024]{3,2,1,0:T(8,128)} %g_ref.7) | copy-start | bytes 786436
  0.6 6.6 %copy-start.1 = (bf16[2,1,64,1024]{3,2,1,0:T(8,128)(2,1)S(1)}, bf16[2,1,64,1024]{3,2,1,0:T(8,128)(2,1)}, u32[]{:S(2)}) copy-start(bf16[2,1,64,1024]{3,2,1,0:T(8,128)(2,1)} %p_ref.5) | copy-start | bytes 786436
  1.8 7.0 %collective-permute-start = (f32[128,128]{1,0:T(8,128)S(1)}, f32[128,128]{1,0:T(8,128)S(1)}, u32[]{:S(2)}, u32[]{:S(2)}) collective-permute-start(f32[128,128]{1,0:T(8,128)S(1)} %get-tuple-element.20), channel_id=1, source_target_pairs={{0,1},{1,2},{2,3},{4,5},{5,6},{6,7},{8,9},{9,10},{10,11},{12,13},{... | collective-permute-start | bytes 196616 | tf_op jit(solution)/shard_map/ppermute | solution.py:453
  5.9 5.0 %collective-permute-start.1 = (f32[128,128]{1,0:T(8,128)S(1)}, f32[128,128]{1,0:T(8,128)S(1)}, u32[]{:S(2)}, u32[]{:S(2)}) collective-permute-start(f32[128,128]{1,0:T(8,128)S(1)} %get-tuple-element.21), channel_id=1, source_target_pairs={{1,0},{2,1},{3,2},{5,4},{6,5},{7,6},{9,8},{10,9},{11,10},{13,12},{... | collective-permute-start | bytes 196616 | tf_op jit(solution)/shard_map/ppermute | solution.py:454
  12.6 15.1 %all-to-all-start = ((f16[8,96,128]{2,1,0:T(8,128)(2,1)}), f16[8,96,128]{2,1,0:T(8,128)(2,1)S(1)}, u32[]{:S(2)}, u32[]{:S(2)}) async-start(f16[8,96,128]{2,1,0:T(8,128)(2,1)} %convert_element_type.24), calls=%async_computation | async-start | bytes 393216 | tf_op jit(solution)/shard_map/all_to_all | solution.py:439
  21.1 6.6 %collective-permute-start.2 = (f32[8,128]{1,0:T(8,128)S(1)}, f32[8,128]{1,0:T(8,128)S(1)}, u32[]{:S(2)}, u32[]{:S(2)}) collective-permute-start(f32[8,128]{1,0:T(8,128)S(1)} %get-tuple-element.31.t_ref), channel_id=1, source_target_pairs={{1,2},{2,1},{3,0},{0,3},{5,6},{6,5},{7,4},{4,7},{9,10},{10,9},{11,... | collective-permute-start | bytes 12296 | tf_op jit(solution)/shard_map/ppermute | solution.py:484
